TPU v7x, 32 devices: a whole 2x2x4 slice. The times are simulated.
32 devices in a mesh: leaf: 8 (over z, x), sub: 4 (over y, core).
Axes of the slice: x: 2, y: 2, z: 4, core: 2. Of those that a mesh axis runs over, the one named last changes fastest.
Arguments:
- points: bfloat16 [96, 64, 512], P('leaf', None, 'sub'), may hold values from -5 to 5
- charges: bfloat16 [96, 8, 512], P('leaf', None, 'sub'), may hold values from -6 to 6
- near_leaf: int32 [96, 32], P('leaf'), may hold values from -1 to 95, as said below
- far_node: int32 [96, 32], P('leaf'), may hold values from 0 to 31
- skel_index: int32 [32, 256], P(('leaf', 'sub')), may hold values from 0 to 1535, as said below
- skel_weight: bfloat16 [32, 8, 256], P(('leaf', 'sub')), may hold values from -12 to 12
Outputs:
- potential: float32 [96, 8, 512], P('leaf', None, 'sub')
Inputs may be any that keep to these rules, and one draw needn't show every extreme that they name: `near_leaf`: entry 0 of the list of leaf l is l itself; every other entry is -1 or a leaf held by another index of leaf. Over the lists of the 12 leaves of one index of leaf no leaf appears twice, and at most 3 distinct leaves of any one other index of leaf appear (leaves k * 12 to k * 12 + 11 belong to index k); every draw reaches 3. `skel_index`: the 256 entries of a row are distinct.
All inputs are finite; a program needn't handle non-finite values.
Results may differ from a plain program's by a relative error of at most 0.0003.
Values may be sent and summed in bfloat16 or wider, within the bound.
A program may use at most 64 MiB of HBM per device.

v0:
```python
import jax
import jax.numpy as jnp
from jax import lax
from jax.sharding import PartitionSpec as P

CAP = 3


RATE_SCALE = 2.5


def kernel_apply(targets, sources, weights):
    target_wide = targets.astype(jnp.float32)
    target_sq = jnp.sum(target_wide * target_wide, axis=0)
    source_sq = jnp.sum(jnp.square(sources.astype(jnp.float32)), axis=1)
    inner_prod = jnp.einsum("dr,mdc->rmc", targets, sources, preferred_element_type=jnp.float32)
    distance = target_sq[:, None, None] + source_sq[None] - 2.0 * inner_prod
    decay_rate = RATE_SCALE / targets.shape[0]
    kernel_block = jnp.exp(-decay_rate * distance)
    return jnp.einsum(
        "rmc,mkc->kr", kernel_block, weights.astype(jnp.float32), precision=lax.Precision.HIGHEST
    )


def shards(points, charges, near_leaf, far_node, skel_index, skel_weight):
    leaf_dev, features, quarter = points.shape
    leaf_count = lax.axis_size("leaf")
    own_index = lax.axis_index("leaf")
    slot_count = CAP
    leaves_all = leaf_count * leaf_dev
    entries = near_leaf.reshape(-1)
    live_flat = entries >= 0
    all_ids = jnp.arange(leaves_all, dtype=jnp.int32)
    lane_ids = jnp.arange(leaf_count, dtype=jnp.int32)
    other_row = lane_ids != own_index
    matches = entries[:, None] == all_ids[None, :]
    wanted = jnp.any(matches, axis=0).reshape(leaf_count, leaf_dev) & other_row[:, None]
    wanted_int = wanted.astype(jnp.int32)
    slot_rank = jnp.cumsum(wanted_int, axis=1) - 1
    asked_mask = lax.all_to_all(wanted_int, "leaf", split_axis=0, concat_axis=0, tiled=True)
    asked_rank = jnp.cumsum(asked_mask, axis=1) - 1
    slot_ids = jnp.arange(slot_count, dtype=jnp.int32)
    selector = (
        (asked_mask[:, None, :] == 1) & (asked_rank[:, None, :] == slot_ids[None, :, None])
    ).astype(jnp.bfloat16)
    send_points = jnp.einsum(
        "dcj,jkq->dckq", selector, points, preferred_element_type=jnp.float32
    ).astype(jnp.bfloat16)
    send_charges = jnp.einsum(
        "dcj,jkq->dckq", selector, charges, preferred_element_type=jnp.float32
    ).astype(jnp.bfloat16)
    got_points, got_charges = (
        lax.all_to_all(send_points, "leaf", split_axis=0, concat_axis=0, tiled=True),
        lax.all_to_all(send_charges, "leaf", split_axis=0, concat_axis=0, tiled=True),
    )
    table_points = jnp.concatenate(
        [points, got_points.reshape(leaf_count * slot_count, features, quarter)], axis=0
    )
    table_charges = jnp.concatenate(
        [charges, got_charges.reshape(leaf_count * slot_count, charges.shape[1], quarter)], axis=0
    )
    slot_pos = leaf_dev + lane_ids[:, None] * slot_count + slot_rank
    local_pos = jnp.broadcast_to(
        jnp.arange(leaf_dev, dtype=jnp.int32)[None, :], (leaf_count, leaf_dev)
    )
    pos_table = jnp.where(other_row[:, None], slot_pos, local_pos).reshape(-1)
    position = jnp.sum(jnp.where(matches, pos_table[None, :], 0), axis=1)
    position = position.reshape(leaf_dev, -1)
    live_mask = live_flat.reshape(leaf_dev, -1)
    whole_targets = lax.all_gather(points, "sub", axis=2, tiled=True)

    def near_targets(pieces):
        target, where_from, alive = pieces
        weights = jnp.where(
            alive[:, None, None], table_charges[where_from], jnp.zeros((), jnp.bfloat16)
        )
        return kernel_apply(target, table_points[where_from], weights)

    partial_value = lax.map(near_targets, (whole_targets, position, live_mask))
    near_term = lax.psum_scatter(partial_value, "sub", scatter_dimension=2, tiled=True)
    node_dev, skel_size = skel_index.shape
    flat_points = jnp.transpose(points, (1, 0, 2)).reshape(features, leaf_dev * quarter)
    picked = jnp.take(flat_points, skel_index.reshape(-1), axis=1)
    skel_points = jnp.transpose(picked.reshape(features, node_dev, skel_size), (1, 0, 2))
    all_skel, all_weight = (
        lax.all_gather(skel_points, ("leaf", "sub"), axis=0, tiled=True),
        lax.all_gather(skel_weight, ("leaf", "sub"), axis=0, tiled=True),
    )

    def far_sum(pieces):
        target, node_list = pieces
        return kernel_apply(target, all_skel[node_list], all_weight[node_list])

    far_term = lax.map(far_sum, (points, far_node))
    return near_term + far_term


def solution(mesh):
    in_specs = (
        P("leaf", None, "sub"),
        P("leaf", None, "sub"),
        P("leaf", None),
        P("leaf", None),
        P(("leaf", "sub"), None),
        P(("leaf", "sub"), None, None),
    )
    out_specs = P("leaf", None, "sub")
    return jax.shard_map(shards, mesh=mesh, in_specs=in_specs, out_specs=out_specs, check_vma=False)
```

profile of v0, /device:TPU:0, one launch (start us, length us, event | category | flops | bytes accessed | tf_op | source)
XLA Modules:
  0.0 407.2 jit_solution(3622828070690735007)
XLA Ops:
  9.1 7.3 %all-to-all-start = ((s32[8,1,12]{2,1,0:T(1,128)}), s32[8,1,12]{2,1,0:T(1,128)S(1)}, u32[]{:S(2)}, u32[]{:S(2)}) async-start(s32[8,1,12]{2,1,0:T(1,128)} %bitcast.13), calls=%async_computation | async-start | bytes 8192 | tf_op jit(solution)/shard_map/all_to_all | solution.py:40
  24.4 4.5 %all-to-all-start.1 = ((bf16[8,3,8,128]{3,2,1,0:T(8,128)(2,1)}), bf16[8,3,8,128]{3,2,1,0:T(8,128)(2,1)S(1)}, u32[]{:S(2)}, u32[]{:S(2)}) async-start(bf16[8,3,8,128]{3,2,1,0:T(8,128)(2,1)} %copy.28), calls=%async_computation.1 | async-start | bytes 98304 | tf_op jit(solution)/shard_map/all_to_all | solution.py:54
  30.9 4.8 %all-to-all-done.1 = bf16[8,3,8,128]{3,2,1,0:T(8,128)(2,1)S(1)} async-done(((bf16[8,3,8,128]{3,2,1,0:T(8,128)(2,1)}), bf16[8,3,8,128]{3,2,1,0:T(8,128)(2,1)S(1)}, u32[]{:S(2)}, u32[]{:S(2)}) %all-to-all-start.1) | async-done | bytes 49184 | tf_op jit(solution)/shard_map/all_to_all | solution.py:54
  35.7 3.5 all-to-all-start.2
  39.2 42.6 %all_gather.10 = bf16[32,8,256]{2,1,0:T(8,128)(2,1)S(1)} all-gather(bf16[1,8,256]{2,1,0:T(8,128)(2,1)} %param.15), channel_id=1, replica_groups=mesh['leaf'=8,'sub'=4] {'leaf','sub'}, dimensions={0}, use_global_device_ids=true | all-gather | bytes 135168 | tf_op jit(solution)/shard_map/all_gather | solution.py:87
  82.5 8.9 %all_gather.9 = bf16[12,64,512]{2,1,0:T(8,128)(2,1)S(1)} all-gather(bf16[12,64,128]{2,1,0:T(8,128)(2,1)} %param.10), channel_id=1, replica_groups=mesh['leaf'=8,'sub'=4] {'sub'}, dimensions={2}, use_global_device_ids=true | all-gather | bytes 983040 | tf_op jit(solution)/shard_map/all_gather | solution.py:70
  91.5 173.4 %while.20 = (s32[]{:T(128)}, f32[12,8,512]{2,1,0:T(8,128)}, pred[12,32]{1,0:T(8,128)(4,1)S(1)}, s32[12,32]{1,0:T(8,128)S(1)}, bf16[36,8,128]{2,1,0:T(8,128)(2,1)...) while((s32[]{:T(128)}, f32[12,8,512]{2,1,0:T(8,128)}, ...), condition=%wide.region_7.8_spmd, body=%wide.region_4.7_spmd.sunk | while | flops 479064672 | bytes 19260740 | solution.py:79
  92.2 4.5 %fusion.87 = f32[512,32,128]{2,0,1:T(8,128)} fusion(bf16[32,64,128]{2,1,0:T(8,128)(2,1)S(1)} %gather_fusion, bf16[12,64,512]{2,1,0:T(8,128)(2,1)S(1)} %get-tuple-element.215, s32[]{:T(128)} %get-tuple-element.202), kind=kOutput, calls=%fused_computation.19.clone.1 | convolution fusion | flops 268435456 | bytes 8978436 | tf_op jit(solution)/shard_map/while/body/eval_jaxpr/dr,mdc->rmc/dot_general | solution.py:16
  97.5 8.5 %fusion.88 = f32[12,8,512]{2,1,0:T(8,128)} fusion(f32[12,8,512]{2,1,0:T(8,128)} %get-tuple-element.203, s32[]{:T(128)} %get-tuple-element.202, f32[512,32,128]{2,0,1:T(8,128)} %fusion.87, f32[32,128]{1,0:T(8,128)S(1)} %multiply_reduce_fusion.8, f32[512]{0:T(512)S(1)} %multiply_reduce_fusion.9, bf16[32,8,128]{2,1,0:T(8,128)(2,1)S(1)} %gather_fusion.1, ...), kind=kOutput, calls=%fused_computation.16.clone.1 | convolution fusion | flops 209747968 | bytes 8489504 | tf_op jit(solution)/shard_map/while/body/eval_jaxpr/rmc,mkc->kr/dot_general | solution.py:20
  106.7 4.5 %fusion.87 = f32[512,32,128]{2,0,1:T(8,128)} fusion(bf16[32,64,128]{2,1,0:T(8,128)(2,1)S(1)} %gather_fusion, bf16[12,64,512]{2,1,0:T(8,128)(2,1)S(1)} %get-tuple-element.215, s32[]{:T(128)} %get-tuple-element.202), kind=kOutput, calls=%fused_computation.19.clone.1 | convolution fusion | flops 268435456 | bytes 8978436 | tf_op jit(solution)/shard_map/while/body/eval_jaxpr/dr,mdc->rmc/dot_general | solution.py:16
  112.0 8.5 %fusion.88 = f32[12,8,512]{2,1,0:T(8,128)} fusion(f32[12,8,512]{2,1,0:T(8,128)} %get-tuple-element.203, s32[]{:T(128)} %get-tuple-element.202, f32[512,32,128]{2,0,1:T(8,128)} %fusion.87, f32[32,128]{1,0:T(8,128)S(1)} %multiply_reduce_fusion.8, f32[512]{0:T(512)S(1)} %multiply_reduce_fusion.9, bf16[32,8,128]{2,1,0:T(8,128)(2,1)S(1)} %gather_fusion.1, ...), kind=kOutput, calls=%fused_computation.16.clone.1 | convolution fusion | flops 209747968 | bytes 8489504 | tf_op jit(solution)/shard_map/while/body/eval_jaxpr/rmc,mkc->kr/dot_general | solution.py:20
  121.1 4.5 %fusion.87 = f32[512,32,128]{2,0,1:T(8,128)} fusion(bf16[32,64,128]{2,1,0:T(8,128)(2,1)S(1)} %gather_fusion, bf16[12,64,512]{2,1,0:T(8,128)(2,1)S(1)} %get-tuple-element.215, s32[]{:T(128)} %get-tuple-element.202), kind=kOutput, calls=%fused_computation.19.clone.1 | convolution fusion | flops 268435456 | bytes 8978436 | tf_op jit(solution)/shard_map/while/body/eval_jaxpr/dr,mdc->rmc/dot_general | solution.py:16
  126.4 8.5 %fusion.88 = f32[12,8,512]{2,1,0:T(8,128)} fusion(f32[12,8,512]{2,1,0:T(8,128)} %get-tuple-element.203, s32[]{:T(128)} %get-tuple-element.202, f32[512,32,128]{2,0,1:T(8,128)} %fusion.87, f32[32,128]{1,0:T(8,128)S(1)} %multiply_reduce_fusion.8, f32[512]{0:T(512)S(1)} %multiply_reduce_fusion.9, bf16[32,8,128]{2,1,0:T(8,128)(2,1)S(1)} %gather_fusion.1, ...), kind=kOutput, calls=%fused_computation.16.clone.1 | convolution fusion | flops 209747968 | bytes 8489504 | tf_op jit(solution)/shard_map/while/body/eval_jaxpr/rmc,mkc->kr/dot_general | solution.py:20
  135.6 4.5 %fusion.87 = f32[512,32,128]{2,0,1:T(8,128)} fusion(bf16[32,64,128]{2,1,0:T(8,128)(2,1)S(1)} %gather_fusion, bf16[12,64,512]{2,1,0:T(8,128)(2,1)S(1)} %get-tuple-element.215, s32[]{:T(128)} %get-tuple-element.202), kind=kOutput, calls=%fused_computation.19.clone.1 | convolution fusion | flops 268435456 | bytes 8978436 | tf_op jit(solution)/shard_map/while/body/eval_jaxpr/dr,mdc->rmc/dot_general | solution.py:16
  140.9 8.5 %fusion.88 = f32[12,8,512]{2,1,0:T(8,128)} fusion(f32[12,8,512]{2,1,0:T(8,128)} %get-tuple-element.203, s32[]{:T(128)} %get-tuple-element.202, f32[512,32,128]{2,0,1:T(8,128)} %fusion.87, f32[32,128]{1,0:T(8,128)S(1)} %multiply_reduce_fusion.8, f32[512]{0:T(512)S(1)} %multiply_reduce_fusion.9, bf16[32,8,128]{2,1,0:T(8,128)(2,1)S(1)} %gather_fusion.1, ...), kind=kOutput, calls=%fused_computation.16.clone.1 | convolution fusion | flops 209747968 | bytes 8489504 | tf_op jit(solution)/shard_map/while/body/eval_jaxpr/rmc,mkc->kr/dot_general | solution.py:20
  150.1 4.5 %fusion.87 = f32[512,32,128]{2,0,1:T(8,128)} fusion(bf16[32,64,128]{2,1,0:T(8,128)(2,1)S(1)} %gather_fusion, bf16[12,64,512]{2,1,0:T(8,128)(2,1)S(1)} %get-tuple-element.215, s32[]{:T(128)} %get-tuple-element.202), kind=kOutput, calls=%fused_computation.19.clone.1 | convolution fusion | flops 268435456 | bytes 8978436 | tf_op jit(solution)/shard_map/while/body/eval_jaxpr/dr,mdc->rmc/dot_general | solution.py:16
  155.3 8.5 %fusion.88 = f32[12,8,512]{2,1,0:T(8,128)} fusion(f32[12,8,512]{2,1,0:T(8,128)} %get-tuple-element.203, s32[]{:T(128)} %get-tuple-element.202, f32[512,32,128]{2,0,1:T(8,128)} %fusion.87, f32[32,128]{1,0:T(8,128)S(1)} %multiply_reduce_fusion.8, f32[512]{0:T(512)S(1)} %multiply_reduce_fusion.9, bf16[32,8,128]{2,1,0:T(8,128)(2,1)S(1)} %gather_fusion.1, ...), kind=kOutput, calls=%fused_computation.16.clone.1 | convolution fusion | flops 209747968 | bytes 8489504 | tf_op jit(solution)/shard_map/while/body/eval_jaxpr/rmc,mkc->kr/dot_general | solution.py:20
  164.5 4.5 %fusion.87 = f32[512,32,128]{2,0,1:T(8,128)} fusion(bf16[32,64,128]{2,1,0:T(8,128)(2,1)S(1)} %gather_fusion, bf16[12,64,512]{2,1,0:T(8,128)(2,1)S(1)} %get-tuple-element.215, s32[]{:T(128)} %get-tuple-element.202), kind=kOutput, calls=%fused_computation.19.clone.1 | convolution fusion | flops 268435456 | bytes 8978436 | tf_op jit(solution)/shard_map/while/body/eval_jaxpr/dr,mdc->rmc/dot_general | solution.py:16
  169.8 8.5 %fusion.88 = f32[12,8,512]{2,1,0:T(8,128)} fusion(f32[12,8,512]{2,1,0:T(8,128)} %get-tuple-element.203, s32[]{:T(128)} %get-tuple-element.202, f32[512,32,128]{2,0,1:T(8,128)} %fusion.87, f32[32,128]{1,0:T(8,128)S(1)} %multiply_reduce_fusion.8, f32[512]{0:T(512)S(1)} %multiply_reduce_fusion.9, bf16[32,8,128]{2,1,0:T(8,128)(2,1)S(1)} %gather_fusion.1, ...), kind=kOutput, calls=%fused_computation.16.clone.1 | convolution fusion | flops 209747968 | bytes 8489504 | tf_op jit(solution)/shard_map/while/body/eval_jaxpr/rmc,mkc->kr/dot_general | solution.py:20
  179.0 4.5 %fusion.87 = f32[512,32,128]{2,0,1:T(8,128)} fusion(bf16[32,64,128]{2,1,0:T(8,128)(2,1)S(1)} %gather_fusion, bf16[12,64,512]{2,1,0:T(8,128)(2,1)S(1)} %get-tuple-element.215, s32[]{:T(128)} %get-tuple-element.202), kind=kOutput, calls=%fused_computation.19.clone.1 | convolution fusion | flops 268435456 | bytes 8978436 | tf_op jit(solution)/shard_map/while/body/eval_jaxpr/dr,mdc->rmc/dot_general | solution.py:16
  184.2 8.5 %fusion.88 = f32[12,8,512]{2,1,0:T(8,128)} fusion(f32[12,8,512]{2,1,0:T(8,128)} %get-tuple-element.203, s32[]{:T(128)} %get-tuple-element.202, f32[512,32,128]{2,0,1:T(8,128)} %fusion.87, f32[32,128]{1,0:T(8,128)S(1)} %multiply_reduce_fusion.8, f32[512]{0:T(512)S(1)} %multiply_reduce_fusion.9, bf16[32,8,128]{2,1,0:T(8,128)(2,1)S(1)} %gather_fusion.1, ...), kind=kOutput, calls=%fused_computation.16.clone.1 | convolution fusion | flops 209747968 | bytes 8489504 | tf_op jit(solution)/shard_map/while/body/eval_jaxpr/rmc,mkc->kr/dot_general | solution.py:20
  193.4 4.5 %fusion.87 = f32[512,32,128]{2,0,1:T(8,128)} fusion(bf16[32,64,128]{2,1,0:T(8,128)(2,1)S(1)} %gather_fusion, bf16[12,64,512]{2,1,0:T(8,128)(2,1)S(1)} %get-tuple-element.215, s32[]{:T(128)} %get-tuple-element.202), kind=kOutput, calls=%fused_computation.19.clone.1 | convolution fusion | flops 268435456 | bytes 8978436 | tf_op jit(solution)/shard_map/while/body/eval_jaxpr/dr,mdc->rmc/dot_general | solution.py:16
  198.7 8.5 %fusion.88 = f32[12,8,512]{2,1,0:T(8,128)} fusion(f32[12,8,512]{2,1,0:T(8,128)} %get-tuple-element.203, s32[]{:T(128)} %get-tuple-element.202, f32[512,32,128]{2,0,1:T(8,128)} %fusion.87, f32[32,128]{1,0:T(8,128)S(1)} %multiply_reduce_fusion.8, f32[512]{0:T(512)S(1)} %multiply_reduce_fusion.9, bf16[32,8,128]{2,1,0:T(8,128)(2,1)S(1)} %gather_fusion.1, ...), kind=kOutput, calls=%fused_computation.16.clone.1 | convolution fusion | flops 209747968 | bytes 8489504 | tf_op jit(solution)/shard_map/while/body/eval_jaxpr/rmc,mkc->kr/dot_general | solution.py:20
  207.9 4.5 %fusion.87 = f32[512,32,128]{2,0,1:T(8,128)} fusion(bf16[32,64,128]{2,1,0:T(8,128)(2,1)S(1)} %gather_fusion, bf16[12,64,512]{2,1,0:T(8,128)(2,1)S(1)} %get-tuple-element.215, s32[]{:T(128)} %get-tuple-element.202), kind=kOutput, calls=%fused_computation.19.clone.1 | convolution fusion | flops 268435456 | bytes 8978436 | tf_op jit(solution)/shard_map/while/body/eval_jaxpr/dr,mdc->rmc/dot_general | solution.py:16
  213.1 8.5 %fusion.88 = f32[12,8,512]{2,1,0:T(8,128)} fusion(f32[12,8,512]{2,1,0:T(8,128)} %get-tuple-element.203, s32[]{:T(128)} %get-tuple-element.202, f32[512,32,128]{2,0,1:T(8,128)} %fusion.87, f32[32,128]{1,0:T(8,128)S(1)} %multiply_reduce_fusion.8, f32[512]{0:T(512)S(1)} %multiply_reduce_fusion.9, bf16[32,8,128]{2,1,0:T(8,128)(2,1)S(1)} %gather_fusion.1, ...), kind=kOutput, calls=%fused_computation.16.clone.1 | convolution fusion | flops 209747968 | bytes 8489504 | tf_op jit(solution)/shard_map/while/body/eval_jaxpr/rmc,mkc->kr/dot_general | solution.py:20
  222.3 4.5 %fusion.87 = f32[512,32,128]{2,0,1:T(8,128)} fusion(bf16[32,64,128]{2,1,0:T(8,128)(2,1)S(1)} %gather_fusion, bf16[12,64,512]{2,1,0:T(8,128)(2,1)S(1)} %get-tuple-element.215, s32[]{:T(128)} %get-tuple-element.202), kind=kOutput, calls=%fused_computation.19.clone.1 | convolution fusion | flops 268435456 | bytes 8978436 | tf_op jit(solution)/shard_map/while/body/eval_jaxpr/dr,mdc->rmc/dot_general | solution.py:16
  227.6 8.5 %fusion.88 = f32[12,8,512]{2,1,0:T(8,128)} fusion(f32[12,8,512]{2,1,0:T(8,128)} %get-tuple-element.203, s32[]{:T(128)} %get-tuple-element.202, f32[512,32,128]{2,0,1:T(8,128)} %fusion.87, f32[32,128]{1,0:T(8,128)S(1)} %multiply_reduce_fusion.8, f32[512]{0:T(512)S(1)} %multiply_reduce_fusion.9, bf16[32,8,128]{2,1,0:T(8,128)(2,1)S(1)} %gather_fusion.1, ...), kind=kOutput, calls=%fused_computation.16.clone.1 | convolution fusion | flops 209747968 | bytes 8489504 | tf_op jit(solution)/shard_map/while/body/eval_jaxpr/rmc,mkc->kr/dot_general | solution.py:20
  236.8 4.5 %fusion.87 = f32[512,32,128]{2,0,1:T(8,128)} fusion(bf16[32,64,128]{2,1,0:T(8,128)(2,1)S(1)} %gather_fusion, bf16[12,64,512]{2,1,0:T(8,128)(2,1)S(1)} %get-tuple-element.215, s32[]{:T(128)} %get-tuple-element.202), kind=kOutput, calls=%fused_computation.19.clone.1 | convolution fusion | flops 268435456 | bytes 8978436 | tf_op jit(solution)/shard_map/while/body/eval_jaxpr/dr,mdc->rmc/dot_general | solution.py:16
  242.0 8.5 %fusion.88 = f32[12,8,512]{2,1,0:T(8,128)} fusion(f32[12,8,512]{2,1,0:T(8,128)} %get-tuple-element.203, s32[]{:T(128)} %get-tuple-element.202, f32[512,32,128]{2,0,1:T(8,128)} %fusion.87, f32[32,128]{1,0:T(8,128)S(1)} %multiply_reduce_fusion.8, f32[512]{0:T(512)S(1)} %multiply_reduce_fusion.9, bf16[32,8,128]{2,1,0:T(8,128)(2,1)S(1)} %gather_fusion.1, ...), kind=kOutput, calls=%fused_computation.16.clone.1 | convolution fusion | flops 209747968 | bytes 8489504 | tf_op jit(solution)/shard_map/while/body/eval_jaxpr/rmc,mkc->kr/dot_general | solution.py:20
  251.2 4.5 %fusion.87 = f32[512,32,128]{2,0,1:T(8,128)} fusion(bf16[32,64,128]{2,1,0:T(8,128)(2,1)S(1)} %gather_fusion, bf16[12,64,512]{2,1,0:T(8,128)(2,1)S(1)} %get-tuple-element.215, s32[]{:T(128)} %get-tuple-element.202), kind=kOutput, calls=%fused_computation.19.clone.1 | convolution fusion | flops 268435456 | bytes 8978436 | tf_op jit(solution)/shard_map/while/body/eval_jaxpr/dr,mdc->rmc/dot_general | solution.py:16
  256.5 8.5 %fusion.88 = f32[12,8,512]{2,1,0:T(8,128)} fusion(f32[12,8,512]{2,1,0:T(8,128)} %get-tuple-element.203, s32[]{:T(128)} %get-tuple-element.202, f32[512,32,128]{2,0,1:T(8,128)} %fusion.87, f32[32,128]{1,0:T(8,128)S(1)} %multiply_reduce_fusion.8, f32[512]{0:T(512)S(1)} %multiply_reduce_fusion.9, bf16[32,8,128]{2,1,0:T(8,128)(2,1)S(1)} %gather_fusion.1, ...), kind=kOutput, calls=%fused_computation.16.clone.1 | convolution fusion | flops 209747968 | bytes 8489504 | tf_op jit(solution)/shard_map/while/body/eval_jaxpr/rmc,mkc->kr/dot_general | solution.py:20
  265.0 133.3 %while.21 = (s32[]{:T(128)}, f32[12,8,128]{2,1,0:T(8,128)S(1)}, s32[12,32]{1,0:T(8,128)}, bf16[32,8,256]{2,1,0:T(8,128)(2,1)S(1)}, bf16[12,64,128]{2,1,0:T(8,128...) while((s32[]{:T(128)}, f32[12,8,128]{2,1,0:T(8,128)S(1)}, s32[12,32]{1,0:T(8,128)}, ...), condition=%wide.region_12.13_spmd, body=%wide.region_9.12_spmd.sunk | while | flops 240665568 | bytes 13084381 | solution.py:94
  271.2 5.0 %fusion.95 = f32[12,8,128]{2,1,0:T(8,128)S(1)} fusion(f32[12,8,128]{2,1,0:T(8,128)S(1)} %get-tuple-element.226, s32[]{:T(128)} %get-tuple-element.225, bf16[32,8,256]{2,1,0:T(8,128)(2,1)S(1)} %gather_fusion.2, f32[128,32,256]{2,0,1:T(8,128)} %fusion.94, f32[32,256]{1,0:T(8,128)S(1)} %multiply_reduce_fusion.10, f32[128]{0:T(128)S(1)} %multiply_reduce_fusion.11), kind=kOutput, calls=%fused_computation.47.clone.1 | convolution fusion | flops 104857600 | bytes 4362756 | tf_op jit(solution)/shard_map/while/body/eval_jaxpr/rmc,mkc->kr/dot_general | solution.py:20
  282.3 5.0 %fusion.95 = f32[12,8,128]{2,1,0:T(8,128)S(1)} fusion(f32[12,8,128]{2,1,0:T(8,128)S(1)} %get-tuple-element.226, s32[]{:T(128)} %get-tuple-element.225, bf16[32,8,256]{2,1,0:T(8,128)(2,1)S(1)} %gather_fusion.2, f32[128,32,256]{2,0,1:T(8,128)} %fusion.94, f32[32,256]{1,0:T(8,128)S(1)} %multiply_reduce_fusion.10, f32[128]{0:T(128)S(1)} %multiply_reduce_fusion.11), kind=kOutput, calls=%fused_computation.47.clone.1 | convolution fusion | flops 104857600 | bytes 4362756 | tf_op jit(solution)/shard_map/while/body/eval_jaxpr/rmc,mkc->kr/dot_general | solution.py:20
  293.4 5.0 %fusion.95 = f32[12,8,128]{2,1,0:T(8,128)S(1)} fusion(f32[12,8,128]{2,1,0:T(8,128)S(1)} %get-tuple-element.226, s32[]{:T(128)} %get-tuple-element.225, bf16[32,8,256]{2,1,0:T(8,128)(2,1)S(1)} %gather_fusion.2, f32[128,32,256]{2,0,1:T(8,128)} %fusion.94, f32[32,256]{1,0:T(8,128)S(1)} %multiply_reduce_fusion.10, f32[128]{0:T(128)S(1)} %multiply_reduce_fusion.11), kind=kOutput, calls=%fused_computation.47.clone.1 | convolution fusion | flops 104857600 | bytes 4362756 | tf_op jit(solution)/shard_map/while/body/eval_jaxpr/rmc,mkc->kr/dot_general | solution.py:20
  300.9 2.7 fusion.94
  304.5 5.0 %fusion.95 = f32[12,8,128]{2,1,0:T(8,128)S(1)} fusion(f32[12,8,128]{2,1,0:T(8,128)S(1)} %get-tuple-element.226, s32[]{:T(128)} %get-tuple-element.225, bf16[32,8,256]{2,1,0:T(8,128)(2,1)S(1)} %gather_fusion.2, f32[128,32,256]{2,0,1:T(8,128)} %fusion.94, f32[32,256]{1,0:T(8,128)S(1)} %multiply_reduce_fusion.10, f32[128]{0:T(128)S(1)} %multiply_reduce_fusion.11), kind=kOutput, calls=%fused_computation.47.clone.1 | convolution fusion | flops 104857600 | bytes 4362756 | tf_op jit(solution)/shard_map/while/body/eval_jaxpr/rmc,mkc->kr/dot_general | solution.py:20
  312.0 2.7 fusion.94
  315.6 5.0 %fusion.95 = f32[12,8,128]{2,1,0:T(8,128)S(1)} fusion(f32[12,8,128]{2,1,0:T(8,128)S(1)} %get-tuple-element.226, s32[]{:T(128)} %get-tuple-element.225, bf16[32,8,256]{2,1,0:T(8,128)(2,1)S(1)} %gather_fusion.2, f32[128,32,256]{2,0,1:T(8,128)} %fusion.94, f32[32,256]{1,0:T(8,128)S(1)} %multiply_reduce_fusion.10, f32[128]{0:T(128)S(1)} %multiply_reduce_fusion.11), kind=kOutput, calls=%fused_computation.47.clone.1 | convolution fusion | flops 104857600 | bytes 4362756 | tf_op jit(solution)/shard_map/while/body/eval_jaxpr/rmc,mkc->kr/dot_general | solution.py:20
  326.7 5.0 %fusion.95 = f32[12,8,128]{2,1,0:T(8,128)S(1)} fusion(f32[12,8,128]{2,1,0:T(8,128)S(1)} %get-tuple-element.226, s32[]{:T(128)} %get-tuple-element.225, bf16[32,8,256]{2,1,0:T(8,128)(2,1)S(1)} %gather_fusion.2, f32[128,32,256]{2,0,1:T(8,128)} %fusion.94, f32[32,256]{1,0:T(8,128)S(1)} %multiply_reduce_fusion.10, f32[128]{0:T(128)S(1)} %multiply_reduce_fusion.11), kind=kOutput, calls=%fused_computation.47.clone.1 | convolution fusion | flops 104857600 | bytes 4362756 | tf_op jit(solution)/shard_map/while/body/eval_jaxpr/rmc,mkc->kr/dot_general | solution.py:20
  334.3 2.7 fusion.94
  337.8 5.0 %fusion.95 = f32[12,8,128]{2,1,0:T(8,128)S(1)} fusion(f32[12,8,128]{2,1,0:T(8,128)S(1)} %get-tuple-element.226, s32[]{:T(128)} %get-tuple-element.225, bf16[32,8,256]{2,1,0:T(8,128)(2,1)S(1)} %gather_fusion.2, f32[128,32,256]{2,0,1:T(8,128)} %fusion.94, f32[32,256]{1,0:T(8,128)S(1)} %multiply_reduce_fusion.10, f32[128]{0:T(128)S(1)} %multiply_reduce_fusion.11), kind=kOutput, calls=%fused_computation.47.clone.1 | convolution fusion | flops 104857600 | bytes 4362756 | tf_op jit(solution)/shard_map/while/body/eval_jaxpr/rmc,mkc->kr/dot_general | solution.py:20
  348.9 5.0 %fusion.95 = f32[12,8,128]{2,1,0:T(8,128)S(1)} fusion(f32[12,8,128]{2,1,0:T(8,128)S(1)} %get-tuple-element.226, s32[]{:T(128)} %get-tuple-element.225, bf16[32,8,256]{2,1,0:T(8,128)(2,1)S(1)} %gather_fusion.2, f32[128,32,256]{2,0,1:T(8,128)} %fusion.94, f32[32,256]{1,0:T(8,128)S(1)} %multiply_reduce_fusion.10, f32[128]{0:T(128)S(1)} %multiply_reduce_fusion.11), kind=kOutput, calls=%fused_computation.47.clone.1 | convolution fusion | flops 104857600 | bytes 4362756 | tf_op jit(solution)/shard_map/while/body/eval_jaxpr/rmc,mkc->kr/dot_general | solution.py:20
  360.0 5.0 %fusion.95 = f32[12,8,128]{2,1,0:T(8,128)S(1)} fusion(f32[12,8,128]{2,1,0:T(8,128)S(1)} %get-tuple-element.226, s32[]{:T(128)} %get-tuple-element.225, bf16[32,8,256]{2,1,0:T(8,128)(2,1)S(1)} %gather_fusion.2, f32[128,32,256]{2,0,1:T(8,128)} %fusion.94, f32[32,256]{1,0:T(8,128)S(1)} %multiply_reduce_fusion.10, f32[128]{0:T(128)S(1)} %multiply_reduce_fusion.11), kind=kOutput, calls=%fused_computation.47.clone.1 | convolution fusion | flops 104857600 | bytes 4362756 | tf_op jit(solution)/shard_map/while/body/eval_jaxpr/rmc,mkc->kr/dot_general | solution.py:20
  367.6 2.7 fusion.94
  371.1 5.0 %fusion.95 = f32[12,8,128]{2,1,0:T(8,128)S(1)} fusion(f32[12,8,128]{2,1,0:T(8,128)S(1)} %get-tuple-element.226, s32[]{:T(128)} %get-tuple-element.225, bf16[32,8,256]{2,1,0:T(8,128)(2,1)S(1)} %gather_fusion.2, f32[128,32,256]{2,0,1:T(8,128)} %fusion.94, f32[32,256]{1,0:T(8,128)S(1)} %multiply_reduce_fusion.10, f32[128]{0:T(128)S(1)} %multiply_reduce_fusion.11), kind=kOutput, calls=%fused_computation.47.clone.1 | convolution fusion | flops 104857600 | bytes 4362756 | tf_op jit(solution)/shard_map/while/body/eval_jaxpr/rmc,mkc->kr/dot_general | solution.py:20
  382.2 5.0 %fusion.95 = f32[12,8,128]{2,1,0:T(8,128)S(1)} fusion(f32[12,8,128]{2,1,0:T(8,128)S(1)} %get-tuple-element.226, s32[]{:T(128)} %get-tuple-element.225, bf16[32,8,256]{2,1,0:T(8,128)(2,1)S(1)} %gather_fusion.2, f32[128,32,256]{2,0,1:T(8,128)} %fusion.94, f32[32,256]{1,0:T(8,128)S(1)} %multiply_reduce_fusion.10, f32[128]{0:T(128)S(1)} %multiply_reduce_fusion.11), kind=kOutput, calls=%fused_computation.47.clone.1 | convolution fusion | flops 104857600 | bytes 4362756 | tf_op jit(solution)/shard_map/while/body/eval_jaxpr/rmc,mkc->kr/dot_general | solution.py:20
  393.3 5.0 %fusion.95 = f32[12,8,128]{2,1,0:T(8,128)S(1)} fusion(f32[12,8,128]{2,1,0:T(8,128)S(1)} %get-tuple-element.226, s32[]{:T(128)} %get-tuple-element.225, bf16[32,8,256]{2,1,0:T(8,128)(2,1)S(1)} %gather_fusion.2, f32[128,32,256]{2,0,1:T(8,128)} %fusion.94, f32[32,256]{1,0:T(8,128)S(1)} %multiply_reduce_fusion.10, f32[128]{0:T(128)S(1)} %multiply_reduce_fusion.11), kind=kOutput, calls=%fused_computation.47.clone.1 | convolution fusion | flops 104857600 | bytes 4362756 | tf_op jit(solution)/shard_map/while/body/eval_jaxpr/rmc,mkc->kr/dot_general | solution.py:20
  (209 shorter events, 93.6 us)
Async XLA Ops:
  7.4 84.1 %copy-start = (bf16[12,64,128]{2,1,0:T(8,128)(2,1)S(1)}, bf16[12,64,128]{2,1,0:T(8,128)(2,1)}, u32[]{:S(2)}) copy-start(bf16[12,64,128]{2,1,0:T(8,128)(2,1)} %param.10) | copy-start | bytes 589828
  7.4 84.1 %copy-start.1 = (bf16[12,8,128]{2,1,0:T(8,128)(2,1)S(1)}, bf16[12,8,128]{2,1,0:T(8,128)(2,1)}, u32[]{:S(2)}) copy-start(bf16[12,8,128]{2,1,0:T(8,128)(2,1)} %param.11) | copy-start | bytes 73732
  9.1 13.6 %all-to-all-start = ((s32[8,1,12]{2,1,0:T(1,128)}), s32[8,1,12]{2,1,0:T(1,128)S(1)}, u32[]{:S(2)}, u32[]{:S(2)}) async-start(s32[8,1,12]{2,1,0:T(1,128)} %bitcast.13), calls=%async_computation | async-start | bytes 8192 | tf_op jit(solution)/shard_map/all_to_all | solution.py:40
  16.3 248.7 %all-gather.2.cloned.1.call-start = ((), (), s32[]{:S(2)}) async-start(), calls=%async_computation.5 | async-start | bytes 1081344 | tf_op jit(solution)/shard_map/all_gather | solution.py:86
  24.4 11.3 %all-to-all-start.1 = ((bf16[8,3,8,128]{3,2,1,0:T(8,128)(2,1)}), bf16[8,3,8,128]{3,2,1,0:T(8,128)(2,1)S(1)}, u32[]{:S(2)}, u32[]{:S(2)}) async-start(bf16[8,3,8,128]{3,2,1,0:T(8,128)(2,1)} %copy.28), calls=%async_computation.1 | async-start | bytes 98304 | tf_op jit(solution)/shard_map/all_to_all | solution.py:54
  35.7 55.7 %all-to-all-start.2 = ((bf16[8,3,64,128]{3,2,1,0:T(8,128)(2,1)}), bf16[8,3,64,128]{3,2,1,0:T(8,128)(2,1)S(1)}, u32[]{:S(2)}, u32[]{:S(2)}) async-start(bf16[8,3,64,128]{3,2,1,0:T(8,128)(2,1)} %copy.30), calls=%async_computation.2 | async-start | bytes 786432 | tf_op jit(solution)/shard_map/all_to_all | solution.py:53
  39.2 359.1 %reduce-scatter.2.cloned.1.call-start = ((), (), s32[]{:S(2)}) async-start(), calls=%async_computation.4 | async-start | bytes 245760 | tf_op jit(solution)/shard_map/reduce_scatter | solution.py:80
Sparse Core Ops, SparseCore 0:
  20.7 56.8 all-gather.1
Sparse Core Ops, SparseCore 1:
  265.1 15.8 reduce-scatter.1
where the time goes:
time: 409 us; the launch traced here: 407 us
  matrix products  250 us (61%)
  blocking collectives  51.5 us (13%)
  local copies, waits for them, and re-layouts  49.3 us (12%)
  other arithmetic  19.5 us (5%)
  starting transfers between devices  15.3 us (4%)
  between operations  15 us (4%)
  waiting for transfers between devices  6.28 us (2%)
    dot_general x24, matrix products, kernel_apply(): jnp.einsum('rmc,mkc->kr', kernel_block, weights.astype(jnp.float32), prec...  162 us
    dot_general x24, matrix products, kernel_apply(): jnp.einsum('dr,mdc->rmc', targets, sources, preferred_element_type=jnp.fl...  86 us
    all_gather x1, blocking collectives, shards(): lax.all_gather(skel_weight, ('leaf', 'sub'), axis=0, tiled=True)  42.6 us
    gather x24, local copies, waits for them, and re-layouts, far_sum(): return kernel_apply(target, all_skel[node_list], all_weight[node_list])  28.9 us
    all_gather x1, blocking collectives, shards(): whole_targets = lax.all_gather(points, 'sub', axis=2, tiled=True)  8.93 us
    select_n x12, other arithmetic, far_sum(): return kernel_apply(target, all_skel[node_list], all_weight[node_list])  8.59 us
  transfers between devices with their start and end apart: 5, of which 2 were waited for; matrix products, arithmetic and copies ran while one was open for 77% of the time, Pallas kernels for 0%

commit v1 on v0

v1 whole, which is shorter than its diff:
```python
import functools
import math

import jax
import jax.numpy as jnp
from jax import lax
from jax.experimental import pallas as pl
from jax.experimental.pallas import tpu as pltpu
from jax.sharding import PartitionSpec as P

CAP = 3
RATE_SCALE = 2.5
ROWS = 80


def split3(x):
    a = x.astype(jnp.bfloat16).astype(jnp.float32)
    b = (x - a).astype(jnp.bfloat16).astype(jnp.float32)
    return a, b, (x - a) - b


def stack_rows(main, first, second):
    rows, width = 16, main.shape[1]
    row_id = lax.broadcasted_iota(jnp.int32, (rows, width), 0)
    extra = jnp.zeros((rows, width), jnp.float32)
    for k, piece in enumerate(tuple(first) + tuple(second)):
        extra = jnp.where(row_id == k, piece, extra)
    pad = jnp.zeros((128 - rows - main.shape[0], width), jnp.float32)
    return jnp.concatenate([main, extra, pad], axis=0)


def compute_kernel(
    owner_ref, count_ref, own_ref, charge_ref, tgt_ref, near_ref, skel_ref, out_ref,
    taug, ysrc, yskel, acc, list_ref
):
    leaf_dev, features, quarter = own_ref.shape
    shares = tgt_ref.shape[0]
    slots = near_ref.shape[0]
    nodes = skel_ref.shape[0]
    skel_size = skel_ref.shape[2]
    coef = -(RATE_SCALE / features) * math.log2(math.e)
    one = jnp.ones((1, 1), jnp.float32)

    def source_rows(block):
        wide = block.astype(jnp.float32)
        sq = split3(jnp.sum(wide * wide, axis=0, keepdims=True))
        return stack_rows(wide, (one, one, one), sq)

    def prep(l, carry):
        for q in range(shares):
            wide = tgt_ref[q, l].astype(jnp.float32)
            sq = split3(jnp.sum(wide * wide, axis=0, keepdims=True))
            taug[l, :, q * quarter : (q + 1) * quarter] = stack_rows(
                -2.0 * wide, sq, (one, one, one)
            ).astype(jnp.bfloat16)
        ysrc[l] = source_rows(own_ref[l]).T.astype(jnp.bfloat16)
        return carry

    lax.fori_loop(0, leaf_dev, prep, 0)

    def prep_near(b, carry):
        ysrc[leaf_dev + b] = source_rows(near_ref[b, :features]).T.astype(jnp.bfloat16)
        return carry

    lax.fori_loop(0, slots, prep_near, 0)

    def prep_skel(n, carry):
        for h in range(skel_size // 128):
            block = skel_ref[n, :features, h * 128 : (h + 1) * 128]
            yskel[n, h * 128 : (h + 1) * 128] = source_rows(block).T.astype(jnp.bfloat16)
        return carry

    lax.fori_loop(0, nodes, prep_skel, 0)

    def item(l, sources, weights):
        parts = []
        half = 2 * quarter
        for h in range(shares * quarter // half):
            dist = jnp.dot(
                sources, taug[l, :, h * half : (h + 1) * half],
                preferred_element_type=jnp.float32,
            )
            kern = jnp.exp2(coef * dist)
            high = kern.astype(jnp.bfloat16)
            low = (kern - high.astype(jnp.float32)).astype(jnp.bfloat16)
            parts.append(
                jnp.dot(weights, high, preferred_element_type=jnp.float32)
                + jnp.dot(weights, low, preferred_element_type=jnp.float32)
            )
        return jnp.concatenate(parts, axis=1)

    def own_step(l, carry):
        acc[l] = item(l, ysrc[l], charge_ref[l])
        return carry

    lax.fori_loop(0, leaf_dev, own_step, 0)

    def scan_near(b, pos):
        list_ref[pos] = b
        return pos + (owner_ref[b] >= 0).astype(jnp.int32)

    live = lax.fori_loop(0, slots, scan_near, 0)

    def near_step(i, carry):
        b = list_ref[i]
        l = owner_ref[b]
        acc[l] += item(l, ysrc[leaf_dev + b], near_ref[b, features : features + 8])
        return carry

    lax.fori_loop(0, live, near_step, 0)

    def scan_far(p, pos):
        list_ref[pos] = p
        return pos + (count_ref[p] > 0).astype(jnp.int32)

    pairs = lax.fori_loop(0, leaf_dev * nodes, scan_far, 0)

    def far_step(i, carry):
        p = list_ref[i]
        l = p // nodes
        n = p - l * nodes
        value = item(l, yskel[n], skel_ref[n, features : features + 8])
        acc[l] += value * count_ref[p].astype(jnp.float32)
        return carry

    lax.fori_loop(0, pairs, far_step, 0)

    for q in range(shares):
        out_ref[q] = acc[:, :, q * quarter : (q + 1) * quarter]


def compute(owner, count, points, charges, targets, near, skel):
    leaf_dev, features, quarter = points.shape
    shares = targets.shape[0]
    slots, nodes, skel_size = near.shape[0], skel.shape[0], skel.shape[2]
    vmem = pl.BlockSpec(memory_space=pltpu.VMEM)
    smem = pl.BlockSpec(memory_space=pltpu.SMEM)
    return pl.pallas_call(
        compute_kernel,
        out_shape=jax.ShapeDtypeStruct((shares, leaf_dev, 8, quarter), jnp.float32),
        in_specs=[smem, smem] + [vmem] * 5,
        out_specs=vmem,
        scratch_shapes=[
            pltpu.VMEM((leaf_dev, 128, shares * quarter), jnp.bfloat16),
            pltpu.VMEM((leaf_dev + slots, quarter, 128), jnp.bfloat16),
            pltpu.VMEM((nodes, skel_size, 128), jnp.bfloat16),
            pltpu.VMEM((leaf_dev, 8, shares * quarter), jnp.float32),
            pltpu.SMEM((max(leaf_dev * nodes, slots) + 1,), jnp.int32),
        ],
        compiler_params=pltpu.CompilerParams(vmem_limit_bytes=56 * 1024 * 1024),
    )(owner, count, points, charges, targets, near, skel)


def plan(near_leaf, far_node, node_dev, leaf_count, shares):
    leaf_dev = near_leaf.shape[0]
    own_index = lax.axis_index("leaf")
    all_ids = jnp.arange(leaf_count * leaf_dev, dtype=jnp.int32)
    leaf_ids = jnp.arange(leaf_dev, dtype=jnp.int32)
    marks = jnp.where(near_leaf[:, :, None] == all_ids, leaf_ids[:, None, None] + 1, 0)
    wanted_by = jnp.max(marks, axis=(0, 1)).reshape(leaf_count, leaf_dev)
    other = jnp.arange(leaf_count, dtype=jnp.int32)[:, None] != own_index
    wanted_by = jnp.where(other, wanted_by, 0)
    want = wanted_by > 0
    before = leaf_ids[:, None] > leaf_ids[None, :]
    rank = jnp.sum(jnp.where(before[None] & want[:, None, :], 1, 0), axis=2)
    slot_ids = jnp.arange(CAP, dtype=jnp.int32)
    hit = want[:, None, :] & (rank[:, None, :] == slot_ids[None, :, None])
    owner = jnp.max(jnp.where(hit, wanted_by[:, None, :], 0), axis=2) - 1
    leaf_of_slot = jnp.max(jnp.where(hit, leaf_ids, 0), axis=2)
    ids = jnp.arange(leaf_count, dtype=jnp.int32) * shares + lax.axis_index("sub")
    ids = (ids[:, None] * node_dev + jnp.arange(node_dev, dtype=jnp.int32)).reshape(-1)
    count = jnp.sum((far_node[:, :, None] == ids).astype(jnp.int32), axis=1)
    return owner.reshape(-1), leaf_of_slot, count.reshape(-1)


def shards(points, charges, near_leaf, far_node, skel_index, skel_weight):
    leaf_dev, features, quarter = points.shape
    leaf_count, shares = lax.axis_size("leaf"), lax.axis_size("sub")
    node_dev, skel_size = skel_index.shape
    owner, leaf_of_slot, count = plan(near_leaf, far_node, node_dev, leaf_count, shares)
    asked = lax.all_to_all(leaf_of_slot, "leaf", split_axis=0, concat_axis=0, tiled=True)
    both = jnp.concatenate(
        [points, charges, jnp.zeros((leaf_dev, ROWS - features - 8, quarter), points.dtype)], axis=1
    )
    send = both[asked.reshape(-1)].reshape(leaf_count, CAP, ROWS, quarter)
    near = lax.all_to_all(send, "leaf", split_axis=0, concat_axis=0, tiled=True)
    near = near.reshape(leaf_count * CAP, ROWS, quarter)
    targets = lax.all_gather(points, "sub", axis=0, tiled=False)
    flat = jnp.transpose(points, (1, 0, 2)).reshape(features, leaf_dev * quarter)
    picked = jnp.take(flat, skel_index.reshape(-1), axis=1)
    picked = jnp.transpose(picked.reshape(features, node_dev, skel_size), (1, 0, 2))
    block = jnp.concatenate(
        [picked, skel_weight, jnp.zeros((node_dev, ROWS - features - 8, skel_size), points.dtype)],
        axis=1,
    )
    skel = lax.all_gather(block, "leaf", axis=0, tiled=True)
    partial = compute(owner, count, points, charges, targets, near, skel)
    return lax.psum_scatter(partial, "sub", scatter_dimension=0, tiled=False)


def solution(mesh):
    in_specs = (
        P("leaf", None, "sub"),
        P("leaf", None, "sub"),
        P("leaf", None),
        P("leaf", None),
        P(("leaf", "sub"), None),
        P(("leaf", "sub"), None, None),
    )
    out_specs = P("leaf", None, "sub")
    return jax.shard_map(shards, mesh=mesh, in_specs=in_specs, out_specs=out_specs, check_vma=False)
```

time: 409 us -> 149 us (0.36)
  matrix products: 250 us -> 0 us
  Pallas kernels: 0 us -> 45.1 us
  local copies, waits for them, and re-layouts: 49.3 us -> 7.73 us
  other arithmetic: 19.5 us -> 4.12 us
  waiting for transfers between devices: 6.28 us -> 19.2 us
    dot_general x50 -> x0, matrix products: 250 us -> none  [the longest x24 162 us: kernel_apply(): jnp.einsum('rmc,mkc->kr', kernel_block, weights.astype(jnp.float32), prec...]
    pallas_call x0 -> x1, Pallas kernels: none -> 45.1 us  [compute(): pl.pallas_call(compute_kernel, out_shape=jax.ShapeDtypeStruct((shares, le...]
    gather x49 -> x2, local copies, waits for them, and re-layouts: 44.6 us -> 2.26 us  [the longest x1 1.41 us: shards(): send = both[asked.reshape(-1)].reshape(leaf_count, CAP, ROWS, quarter)]
    reduce_scatter x1, waiting for transfers between devices: 0.01 us -> 18.7 us  [shards(): return lax.psum_scatter(partial, 'sub', scatter_dimension=0, tiled=False)]
    select_n x27 -> x3, other arithmetic: 9.54 us -> 0.79 us  [the longest x2 0.79 us: shards(): picked = jnp.take(flat, skel_index.reshape(-1), axis=1)]
    all_to_all x3 -> x2, waiting for transfers between devices: 6.23 us -> 0.47 us  [the longest x1 0.46 us: shards(): lax.all_to_all(leaf_of_slot, 'leaf', split_axis=0, concat_axis=0, tiled=T...]
    reduce_sum x49 -> x2, other arithmetic: 5.62 us -> 1.33 us  [the longest x1 1.04 us: plan(): count = jnp.sum((far_node[:, :, None] == ids).astype(jnp.int32), axis=1)]
    all_to_all x3 -> x2, starting transfers between devices: 15.2 us -> 12.8 us  [the longest x1 7.25 us: shards(): lax.all_to_all(leaf_of_slot, 'leaf', split_axis=0, concat_axis=0, tiled=T...]
  transfers between devices with their start and end apart: 5 -> 3, of which waited for: 2 -> 2; matrix products, arithmetic and copies ran while one was open for 77% -> 4% of each run, Pallas kernels for 0% -> 0%
where the time goes in v1:
time: 149 us; the launch traced here: 150 us
  blocking collectives  47.6 us (32%)
  Pallas kernels  45.1 us (30%)
  waiting for transfers between devices  19.2 us (13%)
  between operations  13.5 us (9%)
  starting transfers between devices  12.8 us (9%)
  local copies, waits for them, and re-layouts  7.73 us (5%)
  other arithmetic  4.12 us (3%)
    pallas_call x1, Pallas kernels, compute(): pl.pallas_call(compute_kernel, out_shape=jax.ShapeDtypeStruct((shares, le...  45.1 us
    all_gather x1, blocking collectives, shards(): skel = lax.all_gather(block, 'leaf', axis=0, tiled=True)  38.5 us
    reduce_scatter x1, waiting for transfers between devices, shards(): return lax.psum_scatter(partial, 'sub', scatter_dimension=0, tiled=False)  18.7 us
    all_gather x1, blocking collectives, shards(): targets = lax.all_gather(points, 'sub', axis=0, tiled=False)  9.06 us
    all_to_all x1, starting transfers between devices, shards(): lax.all_to_all(leaf_of_slot, 'leaf', split_axis=0, concat_axis=0, tiled=T...  7.25 us
    all_to_all x1, starting transfers between devices, shards(): near = lax.all_to_all(send, 'leaf', split_axis=0, concat_axis=0, tiled=True)  5.53 us
  transfers between devices with their start and end apart: 3, of which 2 were waited for; matrix products, arithmetic and copies ran while one was open for 4% of the time, Pallas kernels for 0%

profile of v1, /device:TPU:0, one launch (start us, length us, event | category | flops | bytes accessed | tf_op | source)
XLA Modules:
  0.0 150.1 jit_solution(5873011840347034006)
XLA Ops:
  6.5 0.0 copy-start.3
  6.5 0.0 copy-start
  6.6 0.7 copy-done.3
  7.2 0.1 select_reduce_fusion
  7.4 0.1 reshape.180
  7.5 0.1 broadcast_compare_fusion
  7.5 0.3 select_reduce_fusion.1
  7.8 0.1 copy.17
  7.9 0.2 select_reduce_fusion.2
  8.1 0.7 copy.19
  8.8 7.3 %all-to-all-start = ((s32[8,1,3]{2,1,0:T(1,128)}), s32[8,1,3]{2,1,0:T(1,128)S(1)}, u32[]{:S(2)}, u32[]{:S(2)}) async-start(s32[8,1,3]{2,1,0:T(1,128)} %copy.19), calls=%async_computation | async-start | bytes 8192 | tf_op jit(solution)/shard_map/all_to_all | solution.py:181
  16.0 0.7 compare_select_fusion
  16.7 0.7 compare_and_fusion
  17.4 0.1 copy.18
  17.5 0.7 sub.6.owner_ref
  18.2 1.0 convert_reduce_fusion
  19.2 0.6 reshape.181.count_ref
  19.8 0.0 copy-start.2
  19.8 0.8 copy.21
  20.7 0.1 pad.5.clone
  20.7 0.0 copy-done
  20.7 0.0 copy-done.2
  20.7 0.1 maximum_maximum_fusion
  20.9 0.2 copy.20
  21.1 0.9 gather_fusion.1
  22.0 0.5 all-to-all-done
  22.4 0.5 broadcast.164
  22.9 0.7 reduce.3
  23.6 0.1 reshape.182
  23.7 1.4 gather_fusion
  25.1 5.5 %all-to-all-start.1 = ((bf16[8,3,80,128]{3,2,1,0:T(8,128)(2,1)}), bf16[8,3,80,128]{3,2,1,0:T(8,128)(2,1)S(1)}, u32[]{:S(2)}, u32[]{:S(2)}) async-start(bf16[8,3,80,128]{3,2,1,0:T(8,128)(2,1)} %bitcast.3), calls=%async_computation.1 | async-start | bytes 983040 | tf_op jit(solution)/shard_map/all_to_all | solution.py:186
  30.6 0.0 reduce-scatter.2.cloned.1.call-start
  30.7 0.1 bitcast_select_fusion
  30.8 0.1 maximum_maximum_fusion.1
  30.9 0.1 copy.22
  31.0 38.5 %all_gather.11.skel_ref = bf16[8,80,256]{2,1,0:T(8,128)(2,1)} all-gather(bf16[1,80,256]{2,1,0:T(8,128)(2,1)S(1)} %copy.22), channel_id=1, replica_groups=mesh['leaf'=8,'sub'=4] {'leaf'}, dimensions={0}, use_global_device_ids=true | all-gather | bytes 368640 | tf_op jit(solution)/shard_map/all_gather | solution.py:196
  69.5 9.1 %all-gather = bf16[48,64,128]{2,1,0:T(8,128)(2,1)} all-gather(bf16[12,64,128]{2,1,0:T(8,128)(2,1)S(1)} %copy-done), channel_id=2, replica_groups=mesh['leaf'=8,'sub'=4] {'sub'}, dimensions={0}, use_global_device_ids=true | all-gather | bytes 983040 | tf_op jit(solution)/shard_map/all_gather | solution.py:188
  78.6 0.0 all-to-all-done.1
  78.6 0.0 copy-start.1
  78.6 0.8 copy-done.1
  79.4 45.1 %shard_map.64 = f32[4,12,8,128]{3,2,1,0:T(8,128)} custom-call(s32[24]{0:T(128)} %sub.6.owner_ref, s32[96]{0:T(128)} %reshape.181.count_ref, bf16[12,64,128]{2,1,0:T(8,128)(2,1)} %own_ref.1, bf16[12,8,128]{2,1,0:T(8,128)(2,1)} %charge_ref.1, bf16[4,12,64,128]{3,2,1,0:T(8,128)(2,1)} %bitcast.17, bf16[24,80,128]{2,1,0:T(8,128)(2,1)} %bitcast.19, ...), custom_call_target="tpu_custom_call" | custom-call | tf_op jit(solution)/shard_map/pallas_call | solution.py:138
  124.5 0.0 reduce-scatter.2.cloned.1.call-update
  124.5 18.7 %reduce-scatter.2.cloned.1.call-done = f32[1,12,8,128]{3,2,1,0:T(8,128)} async-done(((f32[4,12,8,128]{3,2,1,0:T(8,128)}), f32[1,12,8,128]{3,2,1,0:T(8,128)}) %reduce-scatter.2.cloned.1.call-update) | async-done | bytes 49168 | tf_op jit(solution)/shard_map/reduce_scatter | solution.py:198
  (9 shorter events, 0.0 us)
Async XLA Ops:
  6.5 0.7 copy-start.3
  6.5 14.2 %copy-start = (bf16[12,64,128]{2,1,0:T(8,128)(2,1)S(1)}, bf16[12,64,128]{2,1,0:T(8,128)(2,1)}, u32[]{:S(2)}) copy-start(bf16[12,64,128]{2,1,0:T(8,128)(2,1)} %own_ref.1) | copy-start | bytes 589828
  8.8 13.6 %all-to-all-start = ((s32[8,1,3]{2,1,0:T(1,128)}), s32[8,1,3]{2,1,0:T(1,128)S(1)}, u32[]{:S(2)}, u32[]{:S(2)}) async-start(s32[8,1,3]{2,1,0:T(1,128)} %copy.19), calls=%async_computation | async-start | bytes 8192 | tf_op jit(solution)/shard_map/all_to_all | solution.py:181
  19.8 0.9 copy-start.2
  25.1 53.5 %all-to-all-start.1 = ((bf16[8,3,80,128]{3,2,1,0:T(8,128)(2,1)}), bf16[8,3,80,128]{3,2,1,0:T(8,128)(2,1)S(1)}, u32[]{:S(2)}, u32[]{:S(2)}) async-start(bf16[8,3,80,128]{3,2,1,0:T(8,128)(2,1)} %bitcast.3), calls=%async_computation.1 | async-start | bytes 983040 | tf_op jit(solution)/shard_map/all_to_all | solution.py:186
  30.6 112.6 %reduce-scatter.2.cloned.1.call-start = ((), (), s32[]{:S(2)}) async-start(), calls=%async_computation.3 | async-start | bytes 245760 | tf_op jit(solution)/shard_map/reduce_scatter | solution.py:198
  78.6 0.8 copy-start.1
Sparse Core Ops, SparseCore 0:
  124.7 18.5 reduce-scatter.1

commit v2 on v1

--- a/solution.py
+++ b/solution.py
@@ -11,6 +11,7 @@
 CAP = 3
 RATE_SCALE = 2.5
 ROWS = 80
+MESH = pl.DeviceIdType.MESH
 
 
 def split3(x):
@@ -151,6 +152,186 @@
     )(owner, count, points, charges, targets, near, skel)
 
 
+def exchange_kernel(
+    leaf_count, shares, points_ref, charge_ref, ask_ref, index_ref, weight_ref,
+    tgt_ref, near_ref, skel_ref,
+    wide, send_buf, asked, tgt_send, tgt_recv, ask_send, ask_recv, near_send, near_recv,
+    skel_send, skel_recv, local_sem
+):
+    leaf_dev, features, quarter = points_ref.shape
+    node_dev, skel_size = index_ref.shape
+    me = lax.axis_index("leaf")
+    part = lax.axis_index("sub")
+
+    barrier = pltpu.get_barrier_semaphore()
+
+    def greet_leaf(o, carry):
+        pl.semaphore_signal(
+            barrier, inc=1, device_id={"leaf": lax.rem(me + o, leaf_count)}, device_id_type=MESH
+        )
+        return carry
+
+    def greet_sub(o, carry):
+        pl.semaphore_signal(
+            barrier, inc=1, device_id={"sub": lax.rem(part + o, shares)}, device_id_type=MESH
+        )
+        return carry
+
+    lax.fori_loop(1, leaf_count, greet_leaf, 0)
+    lax.fori_loop(1, shares, greet_sub, 0)
+    pl.semaphore_wait(barrier, leaf_count + shares - 2)
+
+    def target_copy(o):
+        return pltpu.make_async_remote_copy(
+            src_ref=points_ref, dst_ref=tgt_ref.at[part],
+            send_sem=tgt_send.at[o], recv_sem=tgt_recv.at[o],
+            device_id={"sub": lax.rem(part + o, shares)}, device_id_type=MESH,
+        )
+
+    def ask_copy(o):
+        k = lax.rem(me + o, leaf_count)
+        return pltpu.make_async_remote_copy(
+            src_ref=ask_ref.at[k], dst_ref=asked.at[o],
+            send_sem=ask_send.at[o], recv_sem=ask_recv.at[o],
+            device_id={"leaf": k}, device_id_type=MESH,
+        )
+
+    def near_copy(o):
+        return pltpu.make_async_remote_copy(
+            src_ref=send_buf.at[o], dst_ref=near_ref.at[me],
+            send_sem=near_send.at[o], recv_sem=near_recv.at[o],
+            device_id={"leaf": lax.rem(me + leaf_count - o, leaf_count)}, device_id_type=MESH,
+        )
+
+    def skel_copy(o):
+        return pltpu.make_async_remote_copy(
+            src_ref=skel_ref.at[me], dst_ref=skel_ref.at[me],
+            send_sem=skel_send.at[o], recv_sem=skel_recv.at[o],
+            device_id={"leaf": lax.rem(me + o, leaf_count)}, device_id_type=MESH,
+        )
+
+    def run(low, high, act):
+        def step(o, carry):
+            act(o)
+            return carry
+
+        lax.fori_loop(low, high, step, 0)
+
+    run(1, leaf_count, lambda o: ask_copy(o).start())
+    run(1, shares, lambda o: target_copy(o).start())
+    own = pltpu.make_async_copy(points_ref, tgt_ref.at[part], local_sem)
+    own.start()
+
+    for i in range(node_dev):
+        index = index_ref[i : i + 1, :]
+        picked = jnp.zeros((features, skel_size), jnp.float32)
+        spot = lax.broadcasted_iota(jnp.int32, (quarter, skel_size), 0)
+        for j in range(leaf_dev):
+            pick = jnp.where(spot + j * quarter == index, 1.0, 0.0).astype(jnp.bfloat16)
+            picked += jnp.dot(points_ref[j], pick, preferred_element_type=jnp.float32)
+        skel_ref[me, i] = jnp.concatenate(
+            [picked, weight_ref[i].astype(jnp.float32),
+             jnp.zeros((ROWS - features - 8, skel_size), jnp.float32)], axis=0
+        ).astype(jnp.bfloat16)
+    run(1, leaf_count, lambda o: skel_copy(o).start())
+
+    for j in range(leaf_dev):
+        wide[j] = jnp.concatenate(
+            [points_ref[j].astype(jnp.float32), charge_ref[j].astype(jnp.float32),
+             jnp.zeros((ROWS - features - 8, quarter), jnp.float32)], axis=0
+        )
+
+    def pack(o):
+        ask_copy(o).wait_recv()
+        for c in range(CAP):
+            row = asked[o, c : c + 1, :]
+            block = wide[0]
+            for j in range(1, leaf_dev):
+                block = jnp.where(row == j, wide[j], block)
+            send_buf[o, c] = block.astype(jnp.bfloat16)
+        near_copy(o).start()
+
+    run(1, leaf_count, pack)
+    own.wait()
+    run(1, leaf_count, lambda o: ask_copy(o).wait_send())
+    run(1, shares, lambda o: target_copy(o).wait())
+    run(1, leaf_count, lambda o: skel_copy(o).wait())
+    run(1, leaf_count, lambda o: near_copy(o).wait())
+
+
+def exchange(points, charges, ask, skel_index, skel_weight, leaf_count, shares):
+    leaf_dev, features, quarter = points.shape
+    node_dev, skel_size = skel_index.shape
+    vmem = pl.BlockSpec(memory_space=pltpu.VMEM)
+    dma = pltpu.SemaphoreType.DMA
+    return pl.pallas_call(
+        functools.partial(exchange_kernel, leaf_count, shares),
+        out_shape=(
+            jax.ShapeDtypeStruct((shares, leaf_dev, features, quarter), jnp.bfloat16),
+            jax.ShapeDtypeStruct((leaf_count, CAP, ROWS, quarter), jnp.bfloat16),
+            jax.ShapeDtypeStruct((leaf_count, node_dev, ROWS, skel_size), jnp.bfloat16),
+        ),
+        in_specs=[vmem] * 5,
+        out_specs=(vmem, vmem, vmem),
+        scratch_shapes=[
+            pltpu.VMEM((leaf_dev, ROWS, quarter), jnp.float32),
+            pltpu.VMEM((leaf_count, CAP, ROWS, quarter), jnp.bfloat16),
+            pltpu.VMEM((leaf_count, 8, 128), jnp.int32),
+            dma((shares,)), dma((shares,)),
+            dma((leaf_count,)), dma((leaf_count,)),
+            dma((leaf_count,)), dma((leaf_count,)),
+            dma((leaf_count,)), dma((leaf_count,)),
+            dma,
+        ],
+        compiler_params=pltpu.CompilerParams(
+            collective_id=0, has_side_effects=True, vmem_limit_bytes=56 * 1024 * 1024
+        ),
+    )(points, charges, ask, skel_index, skel_weight)
+
+
+def reduce_kernel(shares, partial_ref, out_ref, held, send_sem, recv_sem):
+    part = lax.axis_index("sub")
+    barrier = pltpu.get_barrier_semaphore()
+    for o in range(1, shares):
+        pl.semaphore_signal(
+            barrier, inc=1, device_id={"sub": lax.rem(part + o, shares)}, device_id_type=MESH
+        )
+    pl.semaphore_wait(barrier, shares - 1)
+    copies = []
+    for o in range(1, shares):
+        other = lax.rem(part + o, shares)
+        copy = pltpu.make_async_remote_copy(
+            src_ref=partial_ref.at[other], dst_ref=held.at[o],
+            send_sem=send_sem.at[o], recv_sem=recv_sem.at[o],
+            device_id={"sub": other}, device_id_type=MESH,
+        )
+        copy.start()
+        copies.append(copy)
+    for copy in copies:
+        copy.wait()
+    total = partial_ref[part]
+    for o in range(1, shares):
+        total += held[o]
+    out_ref[...] = total
+
+
+def reduce_parts(partial):
+    shares = partial.shape[0]
+    vmem = pl.BlockSpec(memory_space=pltpu.VMEM)
+    return pl.pallas_call(
+        functools.partial(reduce_kernel, shares),
+        out_shape=jax.ShapeDtypeStruct(partial.shape[1:], jnp.float32),
+        in_specs=[vmem],
+        out_specs=vmem,
+        scratch_shapes=[
+            pltpu.VMEM(partial.shape, jnp.float32),
+            pltpu.SemaphoreType.DMA((shares,)),
+            pltpu.SemaphoreType.DMA((shares,)),
+        ],
+        compiler_params=pltpu.CompilerParams(collective_id=1, has_side_effects=True),
+    )(partial)
+
+
 def plan(near_leaf, far_node, node_dev, leaf_count, shares):
     leaf_dev = near_leaf.shape[0]
     own_index = lax.axis_index("leaf")
@@ -178,24 +359,15 @@
     leaf_count, shares = lax.axis_size("leaf"), lax.axis_size("sub")
     node_dev, skel_size = skel_index.shape
     owner, leaf_of_slot, count = plan(near_leaf, far_node, node_dev, leaf_count, shares)
-    asked = lax.all_to_all(leaf_of_slot, "leaf", split_axis=0, concat_axis=0, tiled=True)
-    both = jnp.concatenate(
-        [points, charges, jnp.zeros((leaf_dev, ROWS - features - 8, quarter), points.dtype)], axis=1
+    ask = jnp.pad(leaf_of_slot, ((0, 0), (0, 8 - CAP)))
+    ask = jnp.broadcast_to(ask[:, :, None], (leaf_count, 8, 128))
+    targets, near, skel = exchange(
+        points, charges, ask, skel_index, skel_weight, leaf_count, shares
     )
-    send = both[asked.reshape(-1)].reshape(leaf_count, CAP, ROWS, quarter)
-    near = lax.all_to_all(send, "leaf", split_axis=0, concat_axis=0, tiled=True)
     near = near.reshape(leaf_count * CAP, ROWS, quarter)
-    targets = lax.all_gather(points, "sub", axis=0, tiled=False)
-    flat = jnp.transpose(points, (1, 0, 2)).reshape(features, leaf_dev * quarter)
-    picked = jnp.take(flat, skel_index.reshape(-1), axis=1)
-    picked = jnp.transpose(picked.reshape(features, node_dev, skel_size), (1, 0, 2))
-    block = jnp.concatenate(
-        [picked, skel_weight, jnp.zeros((node_dev, ROWS - features - 8, skel_size), points.dtype)],
-        axis=1,
-    )
-    skel = lax.all_gather(block, "leaf", axis=0, tiled=True)
+    skel = skel.reshape(leaf_count * node_dev, ROWS, skel_size)
     partial = compute(owner, count, points, charges, targets, near, skel)
-    return lax.psum_scatter(partial, "sub", scatter_dimension=0, tiled=False)
+    return reduce_parts(partial)
 
 
 def solution(mesh):

time: 149 us -> 88.3 us (0.59); the launches traced: 150 us -> 87.3 us
  blocking collectives: 47.6 us -> 0 us
  Pallas kernels: 45.1 us -> 81.7 us
  waiting for transfers between devices: 19.2 us -> 0 us
  between operations: 13.5 us -> 0.05 us
  starting transfers between devices: 12.8 us -> 0 us
  local copies, waits for them, and re-layouts: 7.73 us -> 4.4 us
  other arithmetic: 4.12 us -> 1.06 us
    all_gather x2 -> x0, blocking collectives: 47.6 us -> none  [the longest x1 38.5 us: shards(): skel = lax.all_gather(block, 'leaf', axis=0, tiled=True)]
    pallas_call x0 -> x2, Pallas kernels: none -> 38.3 us  [the longest x1 28.8 us: exchange(): pl.pallas_call(functools.partial(exchange_kernel, leaf_count, shares), ou...]
    reduce_scatter x1 -> x0, waiting for transfers between devices: 18.7 us -> none  [shards(): return lax.psum_scatter(partial, 'sub', scatter_dimension=0, tiled=False)]
    all_to_all x2 -> x0, starting transfers between devices: 12.8 us -> none  [the longest x1 7.25 us: shards(): lax.all_to_all(leaf_of_slot, 'leaf', split_axis=0, concat_axis=0, tiled=T...]
    gather x2 -> x0, local copies, waits for them, and re-layouts: 2.26 us -> none  [the longest x1 1.41 us: shards(): send = both[asked.reshape(-1)].reshape(leaf_count, CAP, ROWS, quarter)]
    pallas_call x1, Pallas kernels: 45.1 us -> 43.4 us  [compute(): pl.pallas_call(compute_kernel, out_shape=jax.ShapeDtypeStruct((shares, le...]
  transfers between devices with their start and end apart: 3 -> 0, of which waited for: 2 -> 0; matrix products, arithmetic and copies ran while one was open for 4% -> 0% of each run, Pallas kernels for 0% -> 0%
where the time goes in v2:
time: 88.3 us; the launch traced here: 87.3 us
  Pallas kernels  81.7 us (93%)
  local copies, waits for them, and re-layouts  4.4 us (5%)
  other arithmetic  1.06 us (1%)
    pallas_call x1, Pallas kernels, compute(): pl.pallas_call(compute_kernel, out_shape=jax.ShapeDtypeStruct((shares, le...  43.4 us
    pallas_call x1, Pallas kernels, exchange(): pl.pallas_call(functools.partial(exchange_kernel, leaf_count, shares), ou...  28.8 us
    pallas_call x1, Pallas kernels, reduce_parts(): pl.pallas_call(functools.partial(reduce_kernel, shares), out_shape=jax.Sh...  9.55 us
    unnamed x6, local copies, waits for them, and re-layouts  2.18 us

profile of v2, /device:TPU:0, one launch (start us, length us, event | category | flops | bytes accessed | tf_op | source)
XLA Modules:
  0.0 87.3 jit_solution(17935262980547892134)
XLA Ops:
  0.0 0.0 copy-start
  0.0 0.7 copy-done
  0.7 0.1 select_reduce_fusion
  0.9 0.1 reshape.78
  0.9 0.1 broadcast_compare_fusion
  1.0 0.3 select_reduce_fusion.1
  1.3 0.1 copy.7
  1.4 0.2 select_reduce_fusion.2
  1.6 0.1 copy.10
  1.7 0.0 copy-start.1
  1.7 0.1 copy.8
  1.8 0.7 sub.6.owner_ref
  2.4 0.0 copy-done.1
  2.4 0.3 convert_reduce_fusion
  2.8 0.6 reshape.79.count_ref
  3.4 0.7 broadcast_in_dim.78.ask_ref
  4.1 28.8 %shard_map.64 = (bf16[4,12,64,128]{3,2,1,0:T(8,128)(2,1)}, bf16[8,3,80,128]{3,2,1,0:T(8,128)(2,1)}, bf16[8,1,80,256]{3,2,1,0:T(8,128)(2,1)}) custom-call(bf16[12,64,128]{2,1,0:T(8,128)(2,1)} %own_ref.1, bf16[12,8,128]{2,1,0:T(8,128)(2,1)} %charge_ref.3, s32[8,8,128]{2,1,0:T(8,128)} %broadcast_in_dim.78.ask_ref, s32[1,256]{1,0:T(1,128)} %index_ref.1, ...), custom_call_target="tpu_custom_call" | custom-call | tf_op jit(solution)/shard_map/pallas_call | solution.py:267
  32.9 43.4 %shard_map.65.partial_ref = f32[4,12,8,128]{3,2,1,0:T(8,128)} custom-call(s32[24]{0:T(128)} %sub.6.owner_ref, s32[96]{0:T(128)} %reshape.79.count_ref, bf16[12,64,128]{2,1,0:T(8,128)(2,1)} %own_ref.1, bf16[12,8,128]{2,1,0:T(8,128)(2,1)} %charge_ref.3, bf16[4,12,64,128]{3,2,1,0:T(8,128)(2,1)} %get-tuple-element.8.tgt_ref, bf16[24,80,128]{2,1,0:T(8,128)(2,1)} %bitcast.2, ...), custom_call_target="tpu_custom_call" | custom-call | tf_op jit(solution)/shard_map/pallas_call | solution.py:139
  76.3 9.6 %shard_map.66 = f32[12,8,128]{2,1,0:T(8,128)} custom-call(f32[4,12,8,128]{3,2,1,0:T(8,128)} %shard_map.65.partial_ref), custom_call_target="tpu_custom_call" | custom-call | tf_op jit(solution)/shard_map/pallas_call | solution.py:321
  85.8 1.4 %copy.12 = f32[12,8,128]{2,1,0:T(8,128)} copy(f32[12,8,128]{2,1,0:T(8,128)} %shard_map.66) | data formatting | bytes 98304
  (6 shorter events, 0.0 us)
Async XLA Ops:
  0.0 0.7 copy-start
  1.7 0.8 copy-start.1

commit v3 on v1

v3 whole, which is shorter than its diff:
```python
import functools
import math

import jax
import jax.numpy as jnp
from jax import lax
from jax.experimental import pallas as pl
from jax.experimental.pallas import tpu as pltpu
from jax.sharding import PartitionSpec as P

CAP = 3
RATE_SCALE = 2.5
ROWS = 80
PREP = 4
NEAR_UNROLL = 4
SLOT_UNROLL = 7
MESH = pl.DeviceIdType.MESH


def split3(x):
    a = x.astype(jnp.bfloat16).astype(jnp.float32)
    b = (x - a).astype(jnp.bfloat16).astype(jnp.float32)
    return a, b, (x - a) - b


def stack_rows(main, first, second):
    rows, width = 16, main.shape[1]
    row_id = lax.broadcasted_iota(jnp.int32, (rows, width), 0)
    extra = jnp.zeros((rows, width), jnp.float32)
    for k, piece in enumerate(tuple(first) + tuple(second)):
        extra = jnp.where(row_id == k, piece, extra)
    pad = jnp.zeros((128 - rows - main.shape[0], width), jnp.float32)
    return jnp.concatenate([main, extra, pad], axis=0)


def fused_kernel(
    leaf_count, shares, owner_ref, count_ref, points_ref, charge_ref, ask_ref, index_ref,
    weight_ref, out_ref, tgt_ref, near_ref, skel_ref, wide, send_buf, asked, taug, yown, ynear,
    yskel, acc, stage, held, tgt_send, tgt_recv, ask_send, ask_recv, near_send, near_recv,
    skel_send, skel_recv, sum_send, sum_recv
):
    leaf_dev, features, quarter = points_ref.shape
    node_dev, skel_size = index_ref.shape
    nodes = leaf_count * node_dev
    coef = -(RATE_SCALE / features) * math.log2(math.e)
    one = jnp.ones((1, 1), jnp.float32)
    me = lax.axis_index("leaf")
    part = lax.axis_index("sub")

    barrier = pltpu.get_barrier_semaphore()

    def greet_leaf(o, carry):
        pl.semaphore_signal(
            barrier, inc=1, device_id={"leaf": lax.rem(me + o, leaf_count)}, device_id_type=MESH
        )
        return carry

    def greet_sub(o, carry):
        pl.semaphore_signal(
            barrier, inc=1, device_id={"sub": lax.rem(part + o, shares)}, device_id_type=MESH
        )
        return carry

    lax.fori_loop(1, leaf_count, greet_leaf, 0)
    lax.fori_loop(1, shares, greet_sub, 0)
    pl.semaphore_wait(barrier, leaf_count + shares - 2)

    def target_copy(o):
        return pltpu.make_async_remote_copy(
            src_ref=points_ref, dst_ref=tgt_ref.at[o],
            send_sem=tgt_send.at[o], recv_sem=tgt_recv.at[o],
            device_id={"sub": lax.rem(part + o, shares)}, device_id_type=MESH,
        )

    def ask_copy(o):
        k = lax.rem(me + o, leaf_count)
        return pltpu.make_async_remote_copy(
            src_ref=ask_ref.at[k], dst_ref=asked.at[o],
            send_sem=ask_send.at[o], recv_sem=ask_recv.at[o],
            device_id={"leaf": k}, device_id_type=MESH,
        )

    def near_copy(o):
        return pltpu.make_async_remote_copy(
            src_ref=send_buf.at[o], dst_ref=near_ref.at[me],
            send_sem=near_send.at[o], recv_sem=near_recv.at[o],
            device_id={"leaf": lax.rem(me + leaf_count - o, leaf_count)}, device_id_type=MESH,
        )

    def skel_copy(o):
        return pltpu.make_async_remote_copy(
            src_ref=skel_ref.at[me], dst_ref=skel_ref.at[me],
            send_sem=skel_send.at[o], recv_sem=skel_recv.at[o],
            device_id={"leaf": lax.rem(me + o, leaf_count)}, device_id_type=MESH,
        )

    def run(low, high, act):
        def step(o, carry):
            act(o)
            return carry

        lax.fori_loop(low, high, step, 0)

    run(1, leaf_count, lambda o: ask_copy(o).start())
    run(1, shares, lambda o: target_copy(o).start())
    for i in range(node_dev):
        index = index_ref[i : i + 1, :]
        picked = jnp.zeros((features, skel_size), jnp.float32)
        spot = lax.broadcasted_iota(jnp.int32, (quarter, skel_size), 0)
        for j in range(leaf_dev):
            pick = jnp.where(spot + j * quarter == index, 1.0, 0.0).astype(jnp.bfloat16)
            picked += jnp.dot(points_ref[j], pick, preferred_element_type=jnp.float32)
        skel_ref[me, i] = jnp.concatenate(
            [picked, weight_ref[i].astype(jnp.float32),
             jnp.zeros((ROWS - features - 8, skel_size), jnp.float32)], axis=0
        ).astype(jnp.bfloat16)
    run(1, leaf_count, lambda o: skel_copy(o).start())

    for j in range(leaf_dev):
        wide[j] = jnp.concatenate(
            [points_ref[j].astype(jnp.float32), charge_ref[j].astype(jnp.float32),
             jnp.zeros((ROWS - features - 8, quarter), jnp.float32)], axis=0
        )


    def pack(o):
        ask_copy(o).wait_recv()
        for c in range(CAP):
            row = asked[o, c : c + 1, :]
            block = wide[0]
            for j in range(1, leaf_dev):
                block = jnp.where(row == j, wide[j], block)
            send_buf[o, c] = block.astype(jnp.bfloat16)
        near_copy(o).start()

    run(1, leaf_count, pack)

    def source_rows(block):
        rows = block.astype(jnp.float32)
        sq = split3(jnp.sum(rows * rows, axis=0, keepdims=True))
        return stack_rows(rows, (one, one, one), sq)

    def prep_targets(o, l, block):
        rows = block.astype(jnp.float32)
        sq = split3(jnp.sum(rows * rows, axis=0, keepdims=True))
        taug[l, :, o * quarter : (o + 1) * quarter] = stack_rows(
            -2.0 * rows, sq, (one, one, one)
        ).astype(jnp.bfloat16)

    def prep_own(l, carry):
        yown[l] = source_rows(points_ref[l]).T.astype(jnp.bfloat16)
        prep_targets(0, l, points_ref[l])
        return carry

    lax.fori_loop(0, leaf_dev, prep_own, 0, unroll=PREP)

    for o in range(1, shares):
        target_copy(o).wait_recv()

    def prep_rest(l, carry):
        for o in range(1, shares):
            prep_targets(o, l, tgt_ref[o, l])
        return carry

    lax.fori_loop(0, leaf_dev, prep_rest, 0, unroll=PREP)

    def item(l, sources, weights):
        parts = []
        half = 2 * quarter
        for h in range(shares * quarter // half):
            dist = jnp.dot(
                sources, taug[l, :, h * half : (h + 1) * half],
                preferred_element_type=jnp.float32,
            )
            kern = jnp.exp2(coef * dist)
            high = kern.astype(jnp.bfloat16)
            low = (kern - high.astype(jnp.float32)).astype(jnp.bfloat16)
            parts.append(
                jnp.dot(weights, high, preferred_element_type=jnp.float32)
                + jnp.dot(weights, low, preferred_element_type=jnp.float32)
            )
        return jnp.concatenate(parts, axis=1)

    def own_step(l, carry):
        acc[l] = item(l, yown[l], charge_ref[l])
        return carry

    lax.fori_loop(0, leaf_dev, own_step, 0, unroll=NEAR_UNROLL)

    def far_step(o, carry):
        @pl.when(o > 0)
        def _():
            skel_copy(o).wait_recv()

        k = lax.rem(me + leaf_count - o, leaf_count)
        for i in range(node_dev):
            for h in range(skel_size // 128):
                block = skel_ref[k, i, :features, h * 128 : (h + 1) * 128]
                yskel[h * 128 : (h + 1) * 128] = source_rows(block).T.astype(jnp.bfloat16)
            weights = skel_ref[k, i, features : features + 8]
            for l in range(leaf_dev):
                times = count_ref[l * nodes + k * node_dev + i].astype(jnp.float32)
                acc[l] += times * item(l, yskel[...], weights)
        return carry

    lax.fori_loop(0, leaf_count, far_step, 0)

    run(1, leaf_count, lambda o: near_copy(o).wait_recv())

    def prep_near(o, carry):
        k = lax.rem(me + o, leaf_count)
        for c in range(CAP):
            ynear[o, c] = source_rows(near_ref[k, c, :features]).T.astype(jnp.bfloat16)
        return carry

    lax.fori_loop(1, leaf_count, prep_near, 0)

    def near_step(o, carry):
        k = lax.rem(me + o, leaf_count)
        found = []
        for c in range(CAP):
            owner = owner_ref[k * CAP + c]
            value = item(
                jnp.maximum(owner, 0), ynear[o, c], near_ref[k, c, features : features + 8]
            )
            found.append((owner, value))
        for l in range(leaf_dev):
            add = jnp.zeros_like(found[0][1])
            for owner, value in found:
                add += jnp.where(owner == l, value, 0.0)
            acc[l] += add
        return carry

    lax.fori_loop(1, leaf_count, near_step, 0, unroll=SLOT_UNROLL)

    def sum_copy(o):
        return pltpu.make_async_remote_copy(
            src_ref=stage.at[o], dst_ref=held.at[o],
            send_sem=sum_send.at[o], recv_sem=sum_recv.at[o],
            device_id={"sub": lax.rem(part + shares - o, shares)}, device_id_type=MESH,
        )

    for o in range(1, shares):
        stage[o] = acc[:, :, o * quarter : (o + 1) * quarter]
        sum_copy(o).start()
    run(1, leaf_count, lambda o: ask_copy(o).wait_send())
    run(1, shares, lambda o: target_copy(o).wait_send())
    run(1, leaf_count, lambda o: skel_copy(o).wait_send())
    run(1, leaf_count, lambda o: near_copy(o).wait_send())
    total = acc[:, :, :quarter]
    for o in range(1, shares):
        sum_copy(o).wait_recv()
        total += held[o]
    out_ref[...] = total
    for o in range(1, shares):
        sum_copy(o).wait_send()


def fused(owner, count, points, charges, ask, skel_index, skel_weight, leaf_count, shares):
    leaf_dev, features, quarter = points.shape
    node_dev, skel_size = skel_index.shape
    vmem = pl.BlockSpec(memory_space=pltpu.VMEM)
    smem = pl.BlockSpec(memory_space=pltpu.SMEM)
    dma = pltpu.SemaphoreType.DMA
    bf16, f32 = jnp.bfloat16, jnp.float32
    return pl.pallas_call(
        functools.partial(fused_kernel, leaf_count, shares),
        out_shape=jax.ShapeDtypeStruct((leaf_dev, 8, quarter), f32),
        in_specs=[smem, smem] + [vmem] * 5,
        out_specs=vmem,
        scratch_shapes=[
            pltpu.VMEM((shares, leaf_dev, features, quarter), bf16),
            pltpu.VMEM((leaf_count, CAP, ROWS, quarter), bf16),
            pltpu.VMEM((leaf_count, node_dev, ROWS, skel_size), bf16),
            pltpu.VMEM((leaf_dev, ROWS, quarter), f32),
            pltpu.VMEM((leaf_count, CAP, ROWS, quarter), bf16),
            pltpu.VMEM((leaf_count, 8, 128), jnp.int32),
            pltpu.VMEM((leaf_dev, 128, shares * quarter), bf16),
            pltpu.VMEM((leaf_dev, quarter, 128), bf16),
            pltpu.VMEM((leaf_count, CAP, quarter, 128), bf16),
            pltpu.VMEM((skel_size, 128), bf16),
            pltpu.VMEM((leaf_dev, 8, shares * quarter), f32),
            pltpu.VMEM((shares, leaf_dev, 8, quarter), f32),
            pltpu.VMEM((shares, leaf_dev, 8, quarter), f32),
            dma((shares,)), dma((shares,)),
            dma((leaf_count,)), dma((leaf_count,)),
            dma((leaf_count,)), dma((leaf_count,)),
            dma((leaf_count,)), dma((leaf_count,)),
            dma((shares,)), dma((shares,)),
        ],
        compiler_params=pltpu.CompilerParams(
            collective_id=0, has_side_effects=True, vmem_limit_bytes=56 * 1024 * 1024
        ),
    )(owner, count, points, charges, ask, skel_index, skel_weight)


def plan(near_leaf, far_node, node_dev, leaf_count, shares):
    leaf_dev = near_leaf.shape[0]
    own_index = lax.axis_index("leaf")
    all_ids = jnp.arange(leaf_count * leaf_dev, dtype=jnp.int32)
    leaf_ids = jnp.arange(leaf_dev, dtype=jnp.int32)
    marks = jnp.where(near_leaf[:, :, None] == all_ids, leaf_ids[:, None, None] + 1, 0)
    wanted_by = jnp.max(marks, axis=(0, 1)).reshape(leaf_count, leaf_dev)
    other = jnp.arange(leaf_count, dtype=jnp.int32)[:, None] != own_index
    wanted_by = jnp.where(other, wanted_by, 0)
    want = wanted_by > 0
    before = leaf_ids[:, None] > leaf_ids[None, :]
    rank = jnp.sum(jnp.where(before[None] & want[:, None, :], 1, 0), axis=2)
    slot_ids = jnp.arange(CAP, dtype=jnp.int32)
    hit = want[:, None, :] & (rank[:, None, :] == slot_ids[None, :, None])
    owner = jnp.max(jnp.where(hit, wanted_by[:, None, :], 0), axis=2) - 1
    leaf_of_slot = jnp.max(jnp.where(hit, leaf_ids, 0), axis=2)
    ids = jnp.arange(leaf_count, dtype=jnp.int32) * shares + lax.axis_index("sub")
    ids = (ids[:, None] * node_dev + jnp.arange(node_dev, dtype=jnp.int32)).reshape(-1)
    count = jnp.sum((far_node[:, :, None] == ids).astype(jnp.int32), axis=1)
    return owner.reshape(-1), leaf_of_slot, count.reshape(-1)


def shards(points, charges, near_leaf, far_node, skel_index, skel_weight):
    leaf_count, shares = lax.axis_size("leaf"), lax.axis_size("sub")
    node_dev = skel_index.shape[0]
    owner, leaf_of_slot, count = plan(near_leaf, far_node, node_dev, leaf_count, shares)
    ask = jnp.pad(leaf_of_slot, ((0, 0), (0, 8 - CAP)))
    ask = jnp.broadcast_to(ask[:, :, None], (leaf_count, 8, 128))
    return fused(
        owner, count, points, charges, ask, skel_index, skel_weight, leaf_count, shares
    )


def solution(mesh):
    in_specs = (
        P("leaf", None, "sub"),
        P("leaf", None, "sub"),
        P("leaf", None),
        P("leaf", None),
        P(("leaf", "sub"), None),
        P(("leaf", "sub"), None, None),
    )
    out_specs = P("leaf", None, "sub")
    return jax.shard_map(shards, mesh=mesh, in_specs=in_specs, out_specs=out_specs, check_vma=False)
```

time: 149 us -> 47.5 us (0.32)
  blocking collectives: 47.6 us -> 0 us
  waiting for transfers between devices: 19.2 us -> 0 us
  between operations: 13.5 us -> 0.05 us
  starting transfers between devices: 12.8 us -> 0 us
  local copies, waits for them, and re-layouts: 7.73 us -> 4.41 us
  Pallas kernels: 45.1 us -> 41.8 us
  other arithmetic: 4.12 us -> 1.06 us
    all_gather x2 -> x0, blocking collectives: 47.6 us -> none  [the longest x1 38.5 us: shards(): skel = lax.all_gather(block, 'leaf', axis=0, tiled=True)]
    reduce_scatter x1 -> x0, waiting for transfers between devices: 18.7 us -> none  [shards(): return lax.psum_scatter(partial, 'sub', scatter_dimension=0, tiled=False)]
    all_to_all x2 -> x0, starting transfers between devices: 12.8 us -> none  [the longest x1 7.25 us: shards(): lax.all_to_all(leaf_of_slot, 'leaf', split_axis=0, concat_axis=0, tiled=T...]
    pallas_call x1, Pallas kernels: 45.1 us -> 41.8 us  [fused(): pl.pallas_call(functools.partial(fused_kernel, leaf_count, shares), out_s...]
    gather x2 -> x0, local copies, waits for them, and re-layouts: 2.26 us -> none  [the longest x1 1.41 us: shards(): send = both[asked.reshape(-1)].reshape(leaf_count, CAP, ROWS, quarter)]
  transfers between devices with their start and end apart: 3 -> 0, of which waited for: 2 -> 0; matrix products, arithmetic and copies ran while one was open for 4% -> 0% of each run, Pallas kernels for 0% -> 0%
where the time goes in v3:
time: 47.5 us; the launch traced here: 47.3 us
  Pallas kernels  41.8 us (88%)
  local copies, waits for them, and re-layouts  4.41 us (9%)
  other arithmetic  1.06 us (2%)
    pallas_call x1, Pallas kernels, fused(): pl.pallas_call(functools.partial(fused_kernel, leaf_count, shares), out_s...  41.8 us
    unnamed x6, local copies, waits for them, and re-layouts  2.18 us

profile of v3, /device:TPU:0, one launch (start us, length us, event | category | flops | bytes accessed | tf_op | source)
XLA Modules:
  0.0 47.3 jit_solution(6257293533862751003)
XLA Ops:
  0.0 0.0 copy-start
  0.0 0.7 %copy-done = s32[12,32]{1,0:T(8,128)S(1)} copy-done((s32[12,32]{1,0:T(8,128)S(1)}, s32[12,32]{1,0:T(8,128)}, u32[]{:S(2)}) %copy-start) | copy-done | bytes 1560
  0.7 0.1 select_reduce_fusion
  0.9 0.1 reshape.72
  0.9 0.1 broadcast_compare_fusion
  1.0 0.3 select_reduce_fusion.1
  1.3 0.1 copy.7
  1.4 0.2 select_reduce_fusion.2
  1.6 0.1 copy.10
  1.7 0.0 copy-start.1
  1.7 0.1 copy.8
  1.8 0.7 %sub.6.owner_ref = s32[24]{0:T(128)} reshape(s32[8,3]{1,0:T(8,128)S(1)} %copy.8) | data formatting | bytes 192 | tf_op jit(solution)/shard_map/sub | solution.py:311
  2.4 0.0 copy-done.1
  2.4 0.3 convert_reduce_fusion
  2.8 0.6 %reshape.73.count_ref = s32[96]{0:T(128)} reshape(s32[12,8]{1,0:T(8,128)S(1)} %convert_reduce_fusion) | data formatting | bytes 768 | tf_op jit(solution)/shard_map/reshape | solution.py:316
  3.4 0.7 %broadcast_in_dim.78.ask_ref = s32[8,8,128]{2,1,0:T(8,128)} broadcast(s32[8,8]{1,0:T(8,128)S(1)} %pad.4.clone), dimensions={0,1} | broadcast | bytes 33024 | tf_op jit(solution)/shard_map/broadcast_in_dim | solution.py:324
  4.1 41.8 %shard_map.64 = f32[12,8,128]{2,1,0:T(8,128)} custom-call(s32[24]{0:T(128)} %sub.6.owner_ref, s32[96]{0:T(128)} %reshape.73.count_ref, bf16[12,64,128]{2,1,0:T(8,128)(2,1)} %points_ref.1, bf16[12,8,128]{2,1,0:T(8,128)(2,1)} %charge_ref.1, s32[8,8,128]{2,1,0:T(8,128)} %broadcast_in_dim.78.ask_ref, s32[1,256]{1,0:T(1,128)} %index_ref.1, ...), custom_call_target="tpu_custom_call" | custom-call | tf_op jit(solution)/shard_map/pallas_call | solution.py:266
  45.9 1.4 %copy.12 = f32[12,8,128]{2,1,0:T(8,128)} copy(f32[12,8,128]{2,1,0:T(8,128)} %shard_map.64) | data formatting | bytes 98304
  (6 shorter events, 0.0 us)
Async XLA Ops:
  0.0 0.7 %copy-start = (s32[12,32]{1,0:T(8,128)S(1)}, s32[12,32]{1,0:T(8,128)}, u32[]{:S(2)}) copy-start(s32[12,32]{1,0:T(8,128)} %param.8) | copy-start | bytes 4612
  1.7 0.8 %copy-start.1 = (s32[12,32]{1,0:T(8,128)S(1)}, s32[12,32]{1,0:T(8,128)}, u32[]{:S(2)}) copy-start(s32[12,32]{1,0:T(8,128)} %param.9) | copy-start | bytes 4612

commit v4 on v3

--- a/solution.py
+++ b/solution.py
@@ -34,14 +34,13 @@
 
 
 def fused_kernel(
-    leaf_count, shares, owner_ref, count_ref, points_ref, charge_ref, ask_ref, index_ref,
-    weight_ref, out_ref, tgt_ref, near_ref, skel_ref, wide, send_buf, asked, taug, yown, ynear,
+    leaf_count, shares, owner_ref, count_ref, slot_ref, points_ref, charge_ref, index_ref,
+    weight_ref, out_ref, ask_ref, tgt_ref, near_ref, skel_ref, wide, send_buf, asked, taug, yown, ynear,
     yskel, acc, stage, held, tgt_send, tgt_recv, ask_send, ask_recv, near_send, near_recv,
     skel_send, skel_recv, sum_send, sum_recv
 ):
     leaf_dev, features, quarter = points_ref.shape
     node_dev, skel_size = index_ref.shape
-    nodes = leaf_count * node_dev
     coef = -(RATE_SCALE / features) * math.log2(math.e)
     one = jnp.ones((1, 1), jnp.float32)
     me = lax.axis_index("leaf")
@@ -61,8 +60,15 @@
         )
         return carry
 
+    def fill_ask(k, carry):
+        for c in range(CAP):
+            ask_ref[k, c : c + 1, :] = jnp.full((1, 128), slot_ref[k, c], jnp.int32)
+        ask_ref[k, CAP:, :] = jnp.zeros((8 - CAP, 128), jnp.int32)
+        return carry
+
     lax.fori_loop(1, leaf_count, greet_leaf, 0)
     lax.fori_loop(1, shares, greet_sub, 0)
+    lax.fori_loop(0, leaf_count, fill_ask, 0)
     pl.semaphore_wait(barrier, leaf_count + shares - 2)
 
     def target_copy(o):
@@ -199,7 +205,7 @@
                 yskel[h * 128 : (h + 1) * 128] = source_rows(block).T.astype(jnp.bfloat16)
             weights = skel_ref[k, i, features : features + 8]
             for l in range(leaf_dev):
-                times = count_ref[l * nodes + k * node_dev + i].astype(jnp.float32)
+                times = count_ref[l, k * node_dev + i].astype(jnp.float32)
                 acc[l] += times * item(l, yskel[...], weights)
         return carry
 
@@ -219,7 +225,7 @@
         k = lax.rem(me + o, leaf_count)
         found = []
         for c in range(CAP):
-            owner = owner_ref[k * CAP + c]
+            owner = owner_ref[k, c]
             value = item(
                 jnp.maximum(owner, 0), ynear[o, c], near_ref[k, c, features : features + 8]
             )
@@ -256,7 +262,7 @@
         sum_copy(o).wait_send()
 
 
-def fused(owner, count, points, charges, ask, skel_index, skel_weight, leaf_count, shares):
+def fused(owner, count, slot_leaf, points, charges, skel_index, skel_weight, leaf_count, shares):
     leaf_dev, features, quarter = points.shape
     node_dev, skel_size = skel_index.shape
     vmem = pl.BlockSpec(memory_space=pltpu.VMEM)
@@ -266,9 +272,10 @@
     return pl.pallas_call(
         functools.partial(fused_kernel, leaf_count, shares),
         out_shape=jax.ShapeDtypeStruct((leaf_dev, 8, quarter), f32),
-        in_specs=[smem, smem] + [vmem] * 5,
+        in_specs=[smem] * 3 + [vmem] * 4,
         out_specs=vmem,
         scratch_shapes=[
+            pltpu.VMEM((leaf_count, 8, 128), jnp.int32),
             pltpu.VMEM((shares, leaf_dev, features, quarter), bf16),
             pltpu.VMEM((leaf_count, CAP, ROWS, quarter), bf16),
             pltpu.VMEM((leaf_count, node_dev, ROWS, skel_size), bf16),
@@ -291,7 +298,7 @@
         compiler_params=pltpu.CompilerParams(
             collective_id=0, has_side_effects=True, vmem_limit_bytes=56 * 1024 * 1024
         ),
-    )(owner, count, points, charges, ask, skel_index, skel_weight)
+    )(owner, count, slot_leaf, points, charges, skel_index, skel_weight)
 
 
 def plan(near_leaf, far_node, node_dev, leaf_count, shares):
@@ -313,17 +320,15 @@
     ids = jnp.arange(leaf_count, dtype=jnp.int32) * shares + lax.axis_index("sub")
     ids = (ids[:, None] * node_dev + jnp.arange(node_dev, dtype=jnp.int32)).reshape(-1)
     count = jnp.sum((far_node[:, :, None] == ids).astype(jnp.int32), axis=1)
-    return owner.reshape(-1), leaf_of_slot, count.reshape(-1)
+    return owner, leaf_of_slot, count
 
 
 def shards(points, charges, near_leaf, far_node, skel_index, skel_weight):
     leaf_count, shares = lax.axis_size("leaf"), lax.axis_size("sub")
     node_dev = skel_index.shape[0]
     owner, leaf_of_slot, count = plan(near_leaf, far_node, node_dev, leaf_count, shares)
-    ask = jnp.pad(leaf_of_slot, ((0, 0), (0, 8 - CAP)))
-    ask = jnp.broadcast_to(ask[:, :, None], (leaf_count, 8, 128))
     return fused(
-        owner, count, points, charges, ask, skel_index, skel_weight, leaf_count, shares
+        owner, count, leaf_of_slot, points, charges, skel_index, skel_weight, leaf_count, shares
     )
 
 

time: 47.5 us -> 47.4 us (level)
  local copies, waits for them, and re-layouts: 4.41 us -> 3.03 us
  other arithmetic: 1.06 us -> 2.26 us
    reduce_max x0 -> x2, local copies, waits for them, and re-layouts: none -> 0.75 us  [the longest x1 0.67 us: plan(): leaf_of_slot = jnp.max(jnp.where(hit, leaf_ids, 0), axis=2)]
    sub x2 -> x0, local copies, waits for them, and re-layouts: 0.74 us -> none  [plan(): owner = jnp.max(jnp.where(hit, wanted_by[:, None, :], 0), axis=2) - 1]
    broadcast_in_dim x1 -> x0, local copies, waits for them, and re-layouts: 0.69 us -> none  [shards(): ask = jnp.broadcast_to(ask[:, :, None], (leaf_count, 8, 128))]
    reshape x1 -> x0, local copies, waits for them, and re-layouts: 0.63 us -> none  [plan(): return (owner.reshape(-1), leaf_of_slot, count.reshape(-1))]
    reduce_sum x1, other arithmetic: 0.34 us -> 0.95 us  [plan(): count = jnp.sum((far_node[:, :, None] == ids).astype(jnp.int32), axis=1)]
    sub x1, other arithmetic: 0.01 us -> 0.6 us  [plan(): owner = jnp.max(jnp.where(hit, wanted_by[:, None, :], 0), axis=2) - 1]
    unnamed x6 -> x5, local copies, waits for them, and re-layouts: 2.18 us -> 2.12 us
where the time goes in v4:
time: 47.4 us; the launch traced here: 47.2 us
  Pallas kernels  41.8 us (88%)
  local copies, waits for them, and re-layouts  3.03 us (6%)
  other arithmetic  2.26 us (5%)
    pallas_call x1, Pallas kernels, fused(): pl.pallas_call(functools.partial(fused_kernel, leaf_count, shares), out_s...  41.8 us
    unnamed x5, local copies, waits for them, and re-layouts  2.12 us

profile of v4, /device:TPU:0, one launch (start us, length us, event | category | flops | bytes accessed | tf_op | source)
XLA Modules:
  0.0 47.2 jit_solution(16141455033046691238)
XLA Ops:
  0.0 0.0 copy-start
  0.0 0.7 %copy-done = s32[12,32]{1,0:T(8,128)S(1)} copy-done((s32[12,32]{1,0:T(8,128)S(1)}, s32[12,32]{1,0:T(8,128)}, u32[]{:S(2)}) %copy-start) | copy-done | bytes 1560
  0.7 0.1 select_reduce_fusion
  0.9 0.1 reshape.64
  0.9 0.1 broadcast_compare_fusion
  1.0 0.3 select_reduce_fusion.1
  1.3 0.1 copy.7
  1.4 0.2 select_reduce_fusion.2
  1.6 0.7 %copy.9.slot_ref = s32[8,3]{1,0:T(8,128)} copy(s32[8,3]{0,1:T(4,128)S(1)} %get-tuple-element.5) | data formatting | bytes 192 | tf_op jit(solution)/shard_map/reduce_max | solution.py:319
  2.2 0.0 copy-start.1
  2.3 0.1 copy.8
  2.3 0.6 %broadcast_add_fusion.owner_ref = s32[8,3]{1,0:T(8,128)} fusion(s32[8,3]{1,0:T(8,128)S(1)} %copy.8), kind=kLoop, calls=%fused_computation.9 | loop fusion | flops 24 | bytes 192 | tf_op jit(solution)/shard_map/sub | solution.py:318
  2.9 0.0 copy-done.1
  2.9 0.9 %convert_reduce_fusion.count_ref = s32[12,8]{1,0:T(8,128)} fusion(s32[12,32]{1,0:T(8,128)S(1)} %copy-done.1, s32[8]{0:T(128)S(1)} %multiply_add_fusion), kind=kLoop, calls=%fused_computation.2 | loop fusion | flops 9120 | bytes 1952 | tf_op jit(solution)/shard_map/reduce_sum | solution.py:322
  3.9 41.8 %shard_map.64 = f32[12,8,128]{2,1,0:T(8,128)} custom-call(s32[8,3]{1,0:T(8,128)} %broadcast_add_fusion.owner_ref, s32[12,8]{1,0:T(8,128)} %convert_reduce_fusion.count_ref, s32[8,3]{1,0:T(8,128)} %copy.9.slot_ref, bf16[12,64,128]{2,1,0:T(8,128)(2,1)} %points_ref.1, bf16[12,8,128]{2,1,0:T(8,128)(2,1)} %charge_ref.1, s32[1,256]{1,0:T(1,128)} %index_ref.1, ...), custom_call_target="tpu_custom_call" | custom-call | tf_op jit(solution)/shard_map/pallas_call | solution.py:272
  45.8 1.4 %copy.11 = f32[12,8,128]{2,1,0:T(8,128)} copy(f32[12,8,128]{2,1,0:T(8,128)} %shard_map.64) | data formatting | bytes 98304
  (4 shorter events, 0.0 us)
Async XLA Ops:
  0.0 0.7 %copy-start = (s32[12,32]{1,0:T(8,128)S(1)}, s32[12,32]{1,0:T(8,128)}, u32[]{:S(2)}) copy-start(s32[12,32]{1,0:T(8,128)} %param.8) | copy-start | bytes 4612
  2.2 0.7 %copy-start.1 = (s32[12,32]{1,0:T(8,128)S(1)}, s32[12,32]{1,0:T(8,128)}, u32[]{:S(2)}) copy-start(s32[12,32]{1,0:T(8,128)} %param.9) | copy-start | bytes 4612

commit v5 on v4

--- a/solution.py
+++ b/solution.py
@@ -12,7 +12,6 @@
 RATE_SCALE = 2.5
 ROWS = 80
 PREP = 4
-NEAR_UNROLL = 4
 SLOT_UNROLL = 7
 MESH = pl.DeviceIdType.MESH
 
@@ -48,6 +47,14 @@
 
     barrier = pltpu.get_barrier_semaphore()
 
+    def flip(o):
+        other, bit = part, 1
+        while bit < shares:
+            if o & bit:
+                other = other + bit - 2 * bit * lax.rem(part // bit, 2)
+            bit *= 2
+        return other
+
     def greet_leaf(o, carry):
         pl.semaphore_signal(
             barrier, inc=1, device_id={"leaf": lax.rem(me + o, leaf_count)}, device_id_type=MESH
@@ -75,7 +82,7 @@
         return pltpu.make_async_remote_copy(
             src_ref=points_ref, dst_ref=tgt_ref.at[o],
             send_sem=tgt_send.at[o], recv_sem=tgt_recv.at[o],
-            device_id={"sub": lax.rem(part + o, shares)}, device_id_type=MESH,
+            device_id={"sub": flip(o)}, device_id_type=MESH,
         )
 
     def ask_copy(o):
@@ -108,7 +115,8 @@
         lax.fori_loop(low, high, step, 0)
 
     run(1, leaf_count, lambda o: ask_copy(o).start())
-    run(1, shares, lambda o: target_copy(o).start())
+    for o in range(shares - 1, 0, -1):
+        target_copy(o).start()
     for i in range(node_dev):
         index = index_ref[i : i + 1, :]
         picked = jnp.zeros((features, skel_size), jnp.float32)
@@ -159,57 +167,63 @@
         return carry
 
     lax.fori_loop(0, leaf_dev, prep_own, 0, unroll=PREP)
-
-    for o in range(1, shares):
-        target_copy(o).wait_recv()
-
-    def prep_rest(l, carry):
-        for o in range(1, shares):
-            prep_targets(o, l, tgt_ref[o, l])
-        return carry
-
-    lax.fori_loop(0, leaf_dev, prep_rest, 0, unroll=PREP)
+    half = shares * quarter // 2
+
+    def item_half(l, h, sources, weights):
+        dist = jnp.dot(
+            sources, taug[l, :, h * half : (h + 1) * half], preferred_element_type=jnp.float32
+        )
+        kern = jnp.exp2(coef * dist)
+        high = kern.astype(jnp.bfloat16)
+        low = (kern - high.astype(jnp.float32)).astype(jnp.bfloat16)
+        return jnp.dot(weights, high, preferred_element_type=jnp.float32) + jnp.dot(
+            weights, low, preferred_element_type=jnp.float32
+        )
 
     def item(l, sources, weights):
-        parts = []
-        half = 2 * quarter
-        for h in range(shares * quarter // half):
-            dist = jnp.dot(
-                sources, taug[l, :, h * half : (h + 1) * half],
-                preferred_element_type=jnp.float32,
-            )
-            kern = jnp.exp2(coef * dist)
-            high = kern.astype(jnp.bfloat16)
-            low = (kern - high.astype(jnp.float32)).astype(jnp.bfloat16)
-            parts.append(
-                jnp.dot(weights, high, preferred_element_type=jnp.float32)
-                + jnp.dot(weights, low, preferred_element_type=jnp.float32)
-            )
-        return jnp.concatenate(parts, axis=1)
-
-    def own_step(l, carry):
-        acc[l] = item(l, yown[l], charge_ref[l])
-        return carry
-
-    lax.fori_loop(0, leaf_dev, own_step, 0, unroll=NEAR_UNROLL)
+        return jnp.concatenate([item_half(l, h, sources, weights) for h in range(2)], axis=1)
+
+    def prep_skel(k, i):
+        for h in range(skel_size // 128):
+            block = skel_ref[k, i, :features, h * 128 : (h + 1) * 128]
+            yskel[h * 128 : (h + 1) * 128] = source_rows(block).T.astype(jnp.bfloat16)
+        return skel_ref[k, i, features : features + 8]
+
+    for h in range(2):
+        fresh = range(max(1, h * shares // 2), (h + 1) * shares // 2)
+        for o in fresh:
+            target_copy(o).wait_recv()
+
+        def prep_part(l, carry):
+            for o in fresh:
+                prep_targets(o, l, tgt_ref[o, l])
+            return carry
+
+        def own_step(l, carry):
+            acc[l, :, h * half : (h + 1) * half] = item_half(l, h, yown[l], charge_ref[l])
+            return carry
+
+        lax.fori_loop(0, leaf_dev, prep_part, 0, unroll=PREP)
+        lax.fori_loop(0, leaf_dev, own_step, 0, unroll=leaf_dev)
+        for i in range(node_dev):
+            weights = prep_skel(me, i)
+            for l in range(leaf_dev):
+                times = count_ref[l, me * node_dev + i].astype(jnp.float32)
+                acc[l, :, h * half : (h + 1) * half] += times * item_half(
+                    l, h, yskel[...], weights
+                )
 
     def far_step(o, carry):
-        @pl.when(o > 0)
-        def _():
-            skel_copy(o).wait_recv()
-
+        skel_copy(o).wait_recv()
         k = lax.rem(me + leaf_count - o, leaf_count)
         for i in range(node_dev):
-            for h in range(skel_size // 128):
-                block = skel_ref[k, i, :features, h * 128 : (h + 1) * 128]
-                yskel[h * 128 : (h + 1) * 128] = source_rows(block).T.astype(jnp.bfloat16)
-            weights = skel_ref[k, i, features : features + 8]
+            weights = prep_skel(k, i)
             for l in range(leaf_dev):
                 times = count_ref[l, k * node_dev + i].astype(jnp.float32)
                 acc[l] += times * item(l, yskel[...], weights)
         return carry
 
-    lax.fori_loop(0, leaf_count, far_step, 0)
+    lax.fori_loop(1, leaf_count, far_step, 0)
 
     run(1, leaf_count, lambda o: near_copy(o).wait_recv())
 
@@ -243,14 +257,15 @@
         return pltpu.make_async_remote_copy(
             src_ref=stage.at[o], dst_ref=held.at[o],
             send_sem=sum_send.at[o], recv_sem=sum_recv.at[o],
-            device_id={"sub": lax.rem(part + shares - o, shares)}, device_id_type=MESH,
+            device_id={"sub": flip(o)}, device_id_type=MESH,
         )
 
     for o in range(1, shares):
         stage[o] = acc[:, :, o * quarter : (o + 1) * quarter]
         sum_copy(o).start()
     run(1, leaf_count, lambda o: ask_copy(o).wait_send())
-    run(1, shares, lambda o: target_copy(o).wait_send())
+    for o in range(1, shares):
+        target_copy(o).wait_send()
     run(1, leaf_count, lambda o: skel_copy(o).wait_send())
     run(1, leaf_count, lambda o: near_copy(o).wait_send())
     total = acc[:, :, :quarter]

time: 47.4 us -> 45.2 us (0.954)
  Pallas kernels: 41.8 us -> 39.7 us
    pallas_call x1, Pallas kernels: 41.8 us -> 39.7 us  [fused(): pl.pallas_call(functools.partial(fused_kernel, leaf_count, shares), out_s...]
where the time goes in v5:
time: 45.2 us; the launch traced here: 45 us
  Pallas kernels  39.7 us (88%)
  local copies, waits for them, and re-layouts  3.03 us (7%)
  other arithmetic  2.26 us (5%)
    pallas_call x1, Pallas kernels, fused(): pl.pallas_call(functools.partial(fused_kernel, leaf_count, shares), out_s...  39.7 us
    unnamed x5, local copies, waits for them, and re-layouts  2.12 us
    reduce_sum x1, other arithmetic, plan(): count = jnp.sum((far_node[:, :, None] == ids).astype(jnp.int32), axis=1)  0.95 us

profile of v5, /device:TPU:0, one launch (start us, length us, event | category | flops | bytes accessed | tf_op | source)
XLA Modules:
  0.0 45.0 jit_solution(8926438948564272591)
XLA Ops:
  0.0 0.0 copy-start
  0.0 0.7 %copy-done = s32[12,32]{1,0:T(8,128)S(1)} copy-done((s32[12,32]{1,0:T(8,128)S(1)}, s32[12,32]{1,0:T(8,128)}, u32[]{:S(2)}) %copy-start) | copy-done | bytes 1560
  0.7 0.1 select_reduce_fusion
  0.9 0.1 reshape.64
  0.9 0.1 broadcast_compare_fusion
  1.0 0.3 select_reduce_fusion.1
  1.3 0.1 copy.7
  1.4 0.2 select_reduce_fusion.2
  1.6 0.7 %copy.9.slot_ref = s32[8,3]{1,0:T(8,128)} copy(s32[8,3]{0,1:T(4,128)S(1)} %get-tuple-element.5) | data formatting | bytes 192 | tf_op jit(solution)/shard_map/reduce_max | solution.py:334
  2.2 0.0 copy-start.1
  2.3 0.1 copy.8
  2.3 0.6 %broadcast_add_fusion.owner_ref = s32[8,3]{1,0:T(8,128)} fusion(s32[8,3]{1,0:T(8,128)S(1)} %copy.8), kind=kLoop, calls=%fused_computation.9 | loop fusion | flops 24 | bytes 192 | tf_op jit(solution)/shard_map/sub | solution.py:333
  2.9 0.0 copy-done.1
  2.9 0.9 %convert_reduce_fusion.count_ref = s32[12,8]{1,0:T(8,128)} fusion(s32[12,32]{1,0:T(8,128)S(1)} %copy-done.1, s32[8]{0:T(128)S(1)} %multiply_add_fusion), kind=kLoop, calls=%fused_computation.2 | loop fusion | flops 9120 | bytes 1952 | tf_op jit(solution)/shard_map/reduce_sum | solution.py:337
  3.9 39.7 %shard_map.64 = f32[12,8,128]{2,1,0:T(8,128)} custom-call(s32[8,3]{1,0:T(8,128)} %broadcast_add_fusion.owner_ref, s32[12,8]{1,0:T(8,128)} %convert_reduce_fusion.count_ref, s32[8,3]{1,0:T(8,128)} %copy.9.slot_ref, bf16[12,64,128]{2,1,0:T(8,128)(2,1)} %points_ref.1, bf16[12,8,128]{2,1,0:T(8,128)(2,1)} %charge_ref.1, s32[1,256]{1,0:T(1,128)} %index_ref.1, ...), custom_call_target="tpu_custom_call" | custom-call | tf_op jit(solution)/shard_map/pallas_call | solution.py:287
  43.6 1.4 %copy.11 = f32[12,8,128]{2,1,0:T(8,128)} copy(f32[12,8,128]{2,1,0:T(8,128)} %shard_map.64) | data formatting | bytes 98304
  (4 shorter events, 0.0 us)
Async XLA Ops:
  0.0 0.7 %copy-start = (s32[12,32]{1,0:T(8,128)S(1)}, s32[12,32]{1,0:T(8,128)}, u32[]{:S(2)}) copy-start(s32[12,32]{1,0:T(8,128)} %param.8) | copy-start | bytes 4612
  2.2 0.7 %copy-start.1 = (s32[12,32]{1,0:T(8,128)S(1)}, s32[12,32]{1,0:T(8,128)}, u32[]{:S(2)}) copy-start(s32[12,32]{1,0:T(8,128)} %param.9) | copy-start | bytes 4612
